TPU v7x, 512 devices: a whole 4x4x16 slice. The times are simulated.
512 devices in a mesh: seq: 64 (over z, y), ch: 8 (over x, core).
Axes of the slice: x: 4, y: 4, z: 16, core: 2. Of those that a mesh axis runs over, the one named last changes fastest.
Arguments:
- query_branch: bfloat16 [16384, 2048], P('seq', 'ch'), may hold values from -6 to 6
- key_branch: bfloat16 [16384, 2048], P('seq', 'ch'), may hold values from -6 to 6
- value_branch: bfloat16 [16384, 2048], P('seq', 'ch'), may hold values from -6 to 6
- short_taps: float32 [3, 7, 2048], P(None, None, 'ch'), may hold values from -2 to 2
- long_taps: float32 [16384, 2048], P('seq', 'ch'), may hold values from -1.5 to 1.5
- skip_gain: float32 [2048], P('ch'), may hold values from 0.5 to 2
Outputs:
- gated_output: bfloat16 [16384, 2048], P('seq', 'ch')
All inputs are finite; a program needn't handle non-finite values.
Results may differ from a plain program's by a relative error of at most 0.001.
Values may be sent and summed in bfloat16 or wider, within the bound.
No kernel may reach another device: no remote copies, remote signals or barrier semaphores. Data moves between devices by JAX's collectives and lax.ppermute only.
A program may use at most 64 MiB of HBM per device.

v0:
```python
import math

import jax
import jax.numpy as jnp
from jax import lax
from jax.sharding import PartitionSpec as P

exact_mode = lax.Precision.HIGHEST
full_turn = 2.0 * math.pi


def from_partner(block, axis, apart):
    count = lax.axis_size(axis)
    route = []
    for low in range(count):
        high = low | 1 << apart
        if high != low and high < count:
            route += [(low, high), (high, low)]
    return lax.ppermute(block, axis, route)


def from_behind(block, axis, distance):
    devices = range(lax.axis_size(axis))
    route = [(i - distance, i) for i in devices if i - distance in devices]
    return lax.ppermute(block, axis, route)


def unit_root(numer, modulus):
    angle = (numer % modulus).astype(jnp.float32) * (-full_turn / modulus)
    return (jnp.cos(angle), jnp.sin(angle))


def complex_apply(mat_real, mat_imag, val_real, val_imag, form):

    def product(left, right):
        return jnp.einsum(form, left, right, precision=exact_mode)

    return (
        product(mat_real, val_real) - product(mat_imag, val_imag),
        product(mat_real, val_imag) + product(mat_imag, val_real),
    )


def rotate(val_real, val_imag, cos_part, sin_part):
    return (val_real * cos_part - val_imag * sin_part, val_real * sin_part + val_imag * cos_part)


def bit_reverse(position, levels):
    result = position * 0
    for bit_place in range(levels):
        result = result + (position >> bit_place & 1) * (1 << levels - 1 - bit_place)
    return result


def square_table(count):
    position = jnp.arange(count, dtype=jnp.int32)
    return unit_root(position[:, None] * position[None, :], count)


def local_forward(val_real, val_imag):
    table_cos, table_sin = square_table(val_real.shape[-2])
    return complex_apply(table_cos, table_sin, val_real, val_imag, "kj,...jc->...kc")


def local_inverse(val_real, val_imag):
    row_count = val_real.shape[-2]
    table_cos, table_sin = square_table(row_count)
    out_real, out_imag = complex_apply(table_cos, -table_sin, val_real, val_imag, "jk,...kc->...jc")
    return (out_real / row_count, out_imag / row_count)


def short_filter(values, rim_part, weights):
    row_count = values.shape[0]
    padded = jnp.concatenate([rim_part, values], axis=0).astype(jnp.float32)
    total = weights[0] * padded[:row_count]
    for offset in range(1, weights.shape[0]):
        total = total + weights[offset] * padded[offset : offset + row_count]
    return total


def forward_pairs(signal):
    dev_count = lax.axis_size("seq")
    dev_index = lax.axis_index("seq")
    levels = dev_count.bit_length() - 1
    row_count = signal.shape[1]
    shift_cos, shift_sin = unit_root(dev_index, 2 * dev_count)
    cur_real = jnp.stack([signal, signal * shift_cos], axis=1)
    cur_imag = jnp.stack([jnp.zeros_like(signal), signal * shift_sin], axis=1)
    for section_bit in reversed(range(levels)):
        half_span = 1 << section_bit
        other_real, other_imag = from_partner((cur_real, cur_imag), "seq", section_bit)
        upper_side = dev_index >> section_bit & 1 == 1
        twist_cos, twist_sin = unit_root(dev_index & half_span - 1, 2 * half_span)
        high_real, high_imag = rotate(
            other_real - cur_real, other_imag - cur_imag, twist_cos, twist_sin
        )
        cur_real = jnp.where(upper_side, high_real, cur_real + other_real)
        cur_imag = jnp.where(upper_side, high_imag, cur_imag + other_imag)
    freq_index = 2 * bit_reverse(dev_index, levels) + jnp.arange(2, dtype=jnp.int32)
    row_index = jnp.arange(row_count, dtype=jnp.int32)
    twist_cos, twist_sin = unit_root(
        freq_index[:, None] * row_index[None, :], 2 * dev_count * row_count
    )
    return rotate(cur_real, cur_imag, twist_cos[None, :, :, None], twist_sin[None, :, :, None])


def inverse_blocks(val_real, val_imag, source_order):
    dev_count = lax.axis_size("seq")
    dev_index = lax.axis_index("seq")
    row_count, channels = (val_real.shape[1], val_real.shape[2])
    piece_rows = row_count // dev_count
    got_real, got_imag = (
        lax.all_to_all(
            val_real.reshape(1, 2, row_count, channels),
            "seq",
            split_axis=2,
            concat_axis=0,
            tiled=True,
        ),
        lax.all_to_all(
            val_imag.reshape(1, 2, row_count, channels),
            "seq",
            split_axis=2,
            concat_axis=0,
            tiled=True,
        ),
    )
    freq_index = 2 * source_order[:, None] + jnp.arange(2, dtype=jnp.int32)[None, :]
    row_index = dev_index * piece_rows + jnp.arange(piece_rows, dtype=jnp.int32)
    twist_cos, twist_sin = unit_root(
        freq_index[:, :, None] * row_index[None, None, :], 2 * dev_count * row_count
    )
    back_real, back_imag = rotate(
        got_real, got_imag, twist_cos[:, :, :, None], -twist_sin[:, :, :, None]
    )
    block_index = jnp.arange(dev_count, dtype=jnp.int32)
    table_cos, table_sin = unit_root(
        block_index[:, None] * freq_index.reshape(-1)[None, :], 2 * dev_count
    )
    flat_real = back_real.reshape(2 * dev_count, piece_rows, channels)
    flat_imag = back_imag.reshape(2 * dev_count, piece_rows, channels)
    blocks = jnp.einsum("bk,kjc->bjc", table_cos, flat_real, precision=exact_mode)
    blocks = (blocks + jnp.einsum("bk,kjc->bjc", table_sin, flat_imag, precision=exact_mode)) / (
        2 * dev_count
    )
    gathered = lax.all_to_all(blocks, "seq", split_axis=0, concat_axis=1, tiled=True)
    return gathered.reshape(row_count, channels)


def shards(query_branch, key_branch, value_branch, short_taps, long_taps, skip_gain):
    margin = short_taps.shape[1] - 1
    rim_rows = from_behind(
        (query_branch[-margin:], key_branch[-margin:], value_branch[-margin:]), "seq", 1
    )
    query_mix = short_filter(query_branch, rim_rows[0], short_taps[0])
    key_mix = short_filter(key_branch, rim_rows[1], short_taps[1])
    value_mix = short_filter(value_branch, rim_rows[2], short_taps[2])
    gated_in = key_mix * value_mix
    signal = jnp.stack([gated_in, long_taps], axis=0)
    dev_count = lax.axis_size("seq")
    spec_real, spec_imag = forward_pairs(signal)
    source_order = bit_reverse(jnp.arange(dev_count, dtype=jnp.int32), dev_count.bit_length() - 1)
    full_real, full_imag = local_forward(spec_real, spec_imag)
    prod_real = full_real[0] * full_real[1] - full_imag[0] * full_imag[1]
    prod_imag = full_real[0] * full_imag[1] + full_imag[0] * full_real[1]
    time_real, time_imag = local_inverse(prod_real, prod_imag)
    long_mix = inverse_blocks(time_real, time_imag, source_order)
    return (query_mix * (long_mix + skip_gain * gated_in)).astype(jnp.bfloat16)


def solution(mesh):
    return jax.shard_map(
        shards,
        mesh=mesh,
        in_specs=(
            P("seq", "ch"),
            P("seq", "ch"),
            P("seq", "ch"),
            P(None, None, "ch"),
            P("seq", "ch"),
            P("ch"),
        ),
        out_specs=P("seq", "ch"),
        check_vma=False,
    )
```

profile of v0, /device:TPU:6, one launch (start us, length us, event | category | flops | bytes accessed | tf_op | source)
XLA Modules:
  0.0 771.1 jit_solution(6187525047425490118)
XLA Ops:
  0.0 0.7 slice.212
  0.7 3.5 collective-permute-start.1
  4.2 0.7 slice.227
  4.9 3.5 collective-permute-start.2
  8.3 1.0 fusion.147
  9.3 0.8 fusion.148
  10.3 1.0 maximum_convert_fusion.1
  12.4 1.1 pad_maximum_fusion
  13.5 18.1 %collective-permute-start.3 = (f32[2,2,256,256]{3,2,1,0:T(8,128)}, f32[2,2,256,256]{3,2,1,0:T(8,128)S(1)}, u32[]{:S(2)}, u32[]{:S(2)}) collective-permute-start(f32[2,2,256,256]{3,2,1,0:T(8,128)} %pad_maximum_fusion), channel_id=1, source_target_pairs={{0,256},{256,0},{8,264},{264,8},{16,272},{272,16},{24,280},{280,24... | collective-permute-start | bytes 3145736 | tf_op jit(solution)/shard_map/ppermute | solution.py:19
  31.6 1.1 stack.34
  32.6 1.9 collective-permute-start.4
  34.7 51.1 %collective-permute-done.3 = f32[2,2,256,256]{3,2,1,0:T(8,128)S(1)} collective-permute-done((f32[2,2,256,256]{3,2,1,0:T(8,128)}, f32[2,2,256,256]{3,2,1,0:T(8,128)S(1)}, u32[]{:S(2)}, u32[]{:S(2)}) %collective-permute-start.3) | collective-permute-done | bytes 1048608 | tf_op jit(solution)/shard_map/ppermute | solution.py:19
  85.8 1.0 copy-done.1
  86.8 122.5 %collective-permute-done.4 = f32[2,2,256,256]{3,2,1,0:T(8,128)} collective-permute-done((f32[2,2,256,256]{3,2,1,0:T(8,128)}, f32[2,2,256,256]{3,2,1,0:T(8,128)}, u32[]{:S(2)}, u32[]{:S(2)}) %collective-permute-start.4) | collective-permute-done | bytes 1048608 | tf_op jit(solution)/shard_map/ppermute | solution.py:19
  209.3 2.9 add_select_fusion.11
  212.3 8.1 %collective-permute-start.5 = (f32[2,2,256,256]{3,2,1,0:T(8,128)S(1)}, f32[2,2,256,256]{3,2,1,0:T(8,128)S(1)}, u32[]{:S(2)}, u32[]{:S(2)}) collective-permute-start(f32[2,2,256,256]{3,2,1,0:T(8,128)S(1)} %get-tuple-element.15), channel_id=1, source_target_pairs={{0,128},{128,0},{8,136},{136,8},{16,144},{144,16},{24,152},{152,24... | collective-permute-start | bytes 3145736 | tf_op jit(solution)/shard_map/ppermute | solution.py:19
  220.4 1.9 collective-permute-start.6
  222.5 145.4 %collective-permute-done.5 = f32[2,2,256,256]{3,2,1,0:T(8,128)S(1)} collective-permute-done((f32[2,2,256,256]{3,2,1,0:T(8,128)S(1)}, f32[2,2,256,256]{3,2,1,0:T(8,128)S(1)}, u32[]{:S(2)}, u32[]{:S(2)}) %collective-permute-start.5) | collective-permute-done | bytes 1048608 | tf_op jit(solution)/shard_map/ppermute | solution.py:19
  367.9 1.0 copy-done.2
  368.9 21.5 %collective-permute-done.6 = f32[2,2,256,256]{3,2,1,0:T(8,128)} collective-permute-done((f32[2,2,256,256]{3,2,1,0:T(8,128)}, f32[2,2,256,256]{3,2,1,0:T(8,128)}, u32[]{:S(2)}, u32[]{:S(2)}) %collective-permute-start.6) | collective-permute-done | bytes 1048608 | tf_op jit(solution)/shard_map/ppermute | solution.py:19
  390.4 3.3 add_select_fusion.9
  393.7 1.9 collective-permute-start.7
  395.6 4.8 collective-permute-start.8
  400.6 65.2 %collective-permute-done.7 = f32[2,2,256,256]{3,2,1,0:T(8,128)S(1)} collective-permute-done((f32[2,2,256,256]{3,2,1,0:T(8,128)S(1)}, f32[2,2,256,256]{3,2,1,0:T(8,128)S(1)}, u32[]{:S(2)}, u32[]{:S(2)}) %collective-permute-start.7) | collective-permute-done | bytes 1048608 | tf_op jit(solution)/shard_map/ppermute | solution.py:19
  465.8 22.5 %collective-permute-done.8 = f32[2,2,256,256]{3,2,1,0:T(8,128)} collective-permute-done((f32[2,2,256,256]{3,2,1,0:T(8,128)}, f32[2,2,256,256]{3,2,1,0:T(8,128)}, u32[]{:S(2)}, u32[]{:S(2)}) %collective-permute-start.8) | collective-permute-done | bytes 1048608 | tf_op jit(solution)/shard_map/ppermute | solution.py:19
  488.3 3.0 add_select_fusion.7
  491.3 1.9 collective-permute-start.10
  493.2 3.9 collective-permute-start.9
  497.3 22.1 %collective-permute-done.10 = f32[2,2,256,256]{3,2,1,0:T(8,128)S(1)} collective-permute-done((f32[2,2,256,256]{3,2,1,0:T(8,128)}, f32[2,2,256,256]{3,2,1,0:T(8,128)S(1)}, u32[]{:S(2)}, u32[]{:S(2)}) %collective-permute-start.10) | collective-permute-done | bytes 1048608 | tf_op jit(solution)/shard_map/ppermute | solution.py:19
  519.4 1.0 copy-done.3
  520.4 20.6 %collective-permute-done.9 = f32[2,2,256,256]{3,2,1,0:T(8,128)} collective-permute-done((f32[2,2,256,256]{3,2,1,0:T(8,128)S(1)}, f32[2,2,256,256]{3,2,1,0:T(8,128)}, u32[]{:S(2)}, u32[]{:S(2)}) %collective-permute-start.9) | collective-permute-done | bytes 1048608 | tf_op jit(solution)/shard_map/ppermute | solution.py:19
  541.0 2.3 add_select_fusion.5
  543.3 2.8 collective-permute-start.11
  546.1 4.5 collective-permute-start.12
  550.9 21.9 %collective-permute-done.11 = f32[2,2,256,256]{3,2,1,0:T(8,128)S(1)} collective-permute-done((f32[2,2,256,256]{3,2,1,0:T(8,128)S(1)}, f32[2,2,256,256]{3,2,1,0:T(8,128)S(1)}, u32[]{:S(2)}, u32[]{:S(2)}) %collective-permute-start.11) | collective-permute-done | bytes 1048608 | tf_op jit(solution)/shard_map/ppermute | solution.py:19
  572.8 1.0 copy-done.4
  573.7 19.8 %collective-permute-done.12 = f32[2,2,256,256]{3,2,1,0:T(8,128)} collective-permute-done((f32[2,2,256,256]{3,2,1,0:T(8,128)S(1)}, f32[2,2,256,256]{3,2,1,0:T(8,128)}, u32[]{:S(2)}, u32[]{:S(2)}) %collective-permute-start.12) | collective-permute-done | bytes 1048608 | tf_op jit(solution)/shard_map/ppermute | solution.py:19
  593.5 2.3 add_select_fusion.3
  595.8 1.9 collective-permute-start.13
  597.8 4.1 collective-permute-start.14
  602.0 21.7 %collective-permute-done.13 = f32[2,2,256,256]{3,2,1,0:T(8,128)S(1)} collective-permute-done((f32[2,2,256,256]{3,2,1,0:T(8,128)S(1)}, f32[2,2,256,256]{3,2,1,0:T(8,128)S(1)}, u32[]{:S(2)}, u32[]{:S(2)}) %collective-permute-start.13) | collective-permute-done | bytes 1048608 | tf_op jit(solution)/shard_map/ppermute | solution.py:19
  623.7 19.9 %collective-permute-done.14 = f32[2,2,256,256]{3,2,1,0:T(8,128)} collective-permute-done((f32[2,2,256,256]{3,2,1,0:T(8,128)S(1)}, f32[2,2,256,256]{3,2,1,0:T(8,128)}, u32[]{:S(2)}, u32[]{:S(2)}) %collective-permute-start.14) | collective-permute-done | bytes 1048608 | tf_op jit(solution)/shard_map/ppermute | solution.py:19
  643.7 1.6 add_select_fusion.1
  645.2 2.8 fusion.21
  648.0 2.8 fusion.20
  650.9 2.8 fusion.1
  653.7 2.8 fusion
  656.6 1.8 fusion.13
  658.4 1.6 fusion.5
  660.0 1.0 copy.46
  661.1 10.8 %all-to-all-start = ((f32[1,2,256,256]{3,1,0,2:T(2,128)}), f32[1,2,256,256]{3,1,0,2:T(2,128)S(1)}, u32[]{:S(2)}, u32[]{:S(2)}) async-start(f32[1,2,256,256]{3,1,0,2:T(2,128)} %copy.46), calls=%async_computation | async-start | bytes 1048576 | tf_op jit(solution)/shard_map/all_to_all | solution.py:113
  671.8 1.6 fusion.9
  673.4 1.6 fusion.3
  675.0 1.0 copy.49
  676.0 26.7 %all-to-all-done = f32[1,2,256,256]{3,1,0,2:T(2,128)S(1)} async-done(((f32[1,2,256,256]{3,1,0,2:T(2,128)}), f32[1,2,256,256]{3,1,0,2:T(2,128)S(1)}, u32[]{:S(2)}, u32[]{:S(2)}) %all-to-all-start) | async-done | bytes 524320 | tf_op jit(solution)/shard_map/all_to_all | solution.py:113
  702.7 5.7 all-to-all-start.1
  709.1 30.6 %all-to-all-done.1 = f32[1,2,256,256]{3,1,0,2:T(2,128)S(1)} async-done(((f32[1,2,256,256]{3,1,0,2:T(2,128)}), f32[1,2,256,256]{3,1,0,2:T(2,128)S(1)}, u32[]{:S(2)}, u32[]{:S(2)}) %all-to-all-start.1) | async-done | bytes 524320 | tf_op jit(solution)/shard_map/all_to_all | solution.py:120
  741.5 0.9 copy.54
  742.3 5.7 all-to-all-start.2
  748.1 3.5 collective-permute-start
  751.6 1.3 collective-permute-done
  752.9 16.5 %all-to-all-done.2 = f32[64,4,256]{2,1,0:T(4,128)S(1)} async-done(((f32[64,4,256]{2,1,0:T(4,128)}), f32[64,4,256]{2,1,0:T(4,128)S(1)}, u32[]{:S(2)}, u32[]{:S(2)}) %all-to-all-start.2) | async-done | bytes 262176 | tf_op jit(solution)/shard_map/all_to_all | solution.py:146
  769.6 0.7 copy-done.8
  770.2 0.9 fusion.40
  (37 shorter events, 3.9 us)
Async XLA Ops:
  0.7 9.6 %collective-permute-start.1 = (bf16[6,256]{1,0:T(8,128)(2,1)S(1)}, bf16[6,256]{1,0:T(8,128)(2,1)S(1)}, u32[]{:S(2)}, u32[]{:S(2)}) collective-permute-start(bf16[6,256]{1,0:T(8,128)(2,1)S(1)} %slice.212), channel_id=1, source_target_pairs={{0,8},{8,16},{16,24},{24,32},{32,40},{40,48},{48,56},{56,64},{64,7... | collective-permute-start | bytes 9224 | tf_op jit(solution)/shard_map/ppermute | solution.py:25
  4.9 6.4 collective-permute-start.2
  10.3 1.0 copy-start.6
  11.3 1.0 copy-start.5
  13.5 72.4 %collective-permute-start.3 = (f32[2,2,256,256]{3,2,1,0:T(8,128)}, f32[2,2,256,256]{3,2,1,0:T(8,128)S(1)}, u32[]{:S(2)}, u32[]{:S(2)}) collective-permute-start(f32[2,2,256,256]{3,2,1,0:T(8,128)} %pad_maximum_fusion), channel_id=1, source_target_pairs={{0,256},{256,0},{8,264},{264,8},{16,272},{272,16},{24,280},{280,24... | collective-permute-start | bytes 3145736 | tf_op jit(solution)/shard_map/ppermute | solution.py:19
  32.6 176.7 %collective-permute-start.4 = (f32[2,2,256,256]{3,2,1,0:T(8,128)}, f32[2,2,256,256]{3,2,1,0:T(8,128)}, u32[]{:S(2)}, u32[]{:S(2)}) collective-permute-start(f32[2,2,256,256]{3,2,1,0:T(8,128)} %stack.34), channel_id=1, source_target_pairs={{0,256},{256,0},{8,264},{264,8},{16,272},{272,16},{24,280},{280,24... | collective-permute-start | bytes 3145736 | tf_op jit(solution)/shard_map/ppermute | solution.py:19
  85.8 1.0 copy-start.1
  212.3 155.7 %collective-permute-start.5 = (f32[2,2,256,256]{3,2,1,0:T(8,128)S(1)}, f32[2,2,256,256]{3,2,1,0:T(8,128)S(1)}, u32[]{:S(2)}, u32[]{:S(2)}) collective-permute-start(f32[2,2,256,256]{3,2,1,0:T(8,128)S(1)} %get-tuple-element.15), channel_id=1, source_target_pairs={{0,128},{128,0},{8,136},{136,8},{16,144},{144,16},{24,152},{152,24... | collective-permute-start | bytes 3145736 | tf_op jit(solution)/shard_map/ppermute | solution.py:19
  220.4 170.0 %collective-permute-start.6 = (f32[2,2,256,256]{3,2,1,0:T(8,128)}, f32[2,2,256,256]{3,2,1,0:T(8,128)}, u32[]{:S(2)}, u32[]{:S(2)}) collective-permute-start(f32[2,2,256,256]{3,2,1,0:T(8,128)} %get-tuple-element.16), channel_id=1, source_target_pairs={{0,128},{128,0},{8,136},{136,8},{16,144},{144,16},{24,152},{152,24... | collective-permute-start | bytes 3145736 | tf_op jit(solution)/shard_map/ppermute | solution.py:19
  367.9 1.0 copy-start.2
  393.7 72.1 %collective-permute-start.7 = (f32[2,2,256,256]{3,2,1,0:T(8,128)S(1)}, f32[2,2,256,256]{3,2,1,0:T(8,128)S(1)}, u32[]{:S(2)}, u32[]{:S(2)}) collective-permute-start(f32[2,2,256,256]{3,2,1,0:T(8,128)S(1)} %get-tuple-element.13), channel_id=1, source_target_pairs={{0,64},{64,0},{8,72},{72,8},{16,80},{80,16},{24,88},{88,24},{32,96... | collective-permute-start | bytes 3145736 | tf_op jit(solution)/shard_map/ppermute | solution.py:19
  395.6 92.7 %collective-permute-start.8 = (f32[2,2,256,256]{3,2,1,0:T(8,128)}, f32[2,2,256,256]{3,2,1,0:T(8,128)}, u32[]{:S(2)}, u32[]{:S(2)}) collective-permute-start(f32[2,2,256,256]{3,2,1,0:T(8,128)} %get-tuple-element.14), channel_id=1, source_target_pairs={{0,64},{64,0},{8,72},{72,8},{16,80},{80,16},{24,88},{88,24},{32,96... | collective-permute-start | bytes 3145736 | tf_op jit(solution)/shard_map/ppermute | solution.py:19
  491.3 28.1 %collective-permute-start.10 = (f32[2,2,256,256]{3,2,1,0:T(8,128)}, f32[2,2,256,256]{3,2,1,0:T(8,128)S(1)}, u32[]{:S(2)}, u32[]{:S(2)}) collective-permute-start(f32[2,2,256,256]{3,2,1,0:T(8,128)} %get-tuple-element.12), channel_id=1, source_target_pairs={{0,32},{32,0},{8,40},{40,8},{16,48},{48,16},{24,56},{56,24},{64,96... | collective-permute-start | bytes 3145736 | tf_op jit(solution)/shard_map/ppermute | solution.py:19
  493.2 47.8 %collective-permute-start.9 = (f32[2,2,256,256]{3,2,1,0:T(8,128)S(1)}, f32[2,2,256,256]{3,2,1,0:T(8,128)}, u32[]{:S(2)}, u32[]{:S(2)}) collective-permute-start(f32[2,2,256,256]{3,2,1,0:T(8,128)S(1)} %get-tuple-element.11), channel_id=1, source_target_pairs={{0,32},{32,0},{8,40},{40,8},{16,48},{48,16},{24,56},{56,24},{64,96... | collective-permute-start | bytes 3145736 | tf_op jit(solution)/shard_map/ppermute | solution.py:19
  519.4 1.0 copy-start.3
  543.3 29.4 %copy-start = (f32[2,2,256,256]{3,2,1,0:T(8,128)}, f32[2,2,256,256]{3,2,1,0:T(8,128)S(1)}, u32[]{:S(2)}) copy-start(f32[2,2,256,256]{3,2,1,0:T(8,128)S(1)} %get-tuple-element.10) | copy-start | bytes 3145732
  543.3 29.4 %collective-permute-start.11 = (f32[2,2,256,256]{3,2,1,0:T(8,128)S(1)}, f32[2,2,256,256]{3,2,1,0:T(8,128)S(1)}, u32[]{:S(2)}, u32[]{:S(2)}) collective-permute-start(f32[2,2,256,256]{3,2,1,0:T(8,128)S(1)} %get-tuple-element.9), channel_id=1, source_target_pairs={{0,16},{16,0},{8,24},{24,8},{32,48},{48,32},{40,56},{56,40},{64,80... | collective-permute-start | bytes 3145736 | tf_op jit(solution)/shard_map/ppermute | solution.py:19
  546.1 47.4 %collective-permute-start.12 = (f32[2,2,256,256]{3,2,1,0:T(8,128)S(1)}, f32[2,2,256,256]{3,2,1,0:T(8,128)}, u32[]{:S(2)}, u32[]{:S(2)}) collective-permute-start(f32[2,2,256,256]{3,2,1,0:T(8,128)S(1)} %get-tuple-element.10), channel_id=1, source_target_pairs={{0,16},{16,0},{8,24},{24,8},{32,48},{48,32},{40,56},{56,40},{64,80... | collective-permute-start | bytes 3145736 | tf_op jit(solution)/shard_map/ppermute | solution.py:19
  572.8 1.0 copy-start.4
  595.8 27.9 %collective-permute-start.13 = (f32[2,2,256,256]{3,2,1,0:T(8,128)S(1)}, f32[2,2,256,256]{3,2,1,0:T(8,128)S(1)}, u32[]{:S(2)}, u32[]{:S(2)}) collective-permute-start(f32[2,2,256,256]{3,2,1,0:T(8,128)S(1)} %get-tuple-element.7), channel_id=1, source_target_pairs={{0,8},{8,0},{16,24},{24,16},{32,40},{40,32},{48,56},{56,48},{64,72... | collective-permute-start | bytes 3145736 | tf_op jit(solution)/shard_map/ppermute | solution.py:19
  597.8 45.9 %collective-permute-start.14 = (f32[2,2,256,256]{3,2,1,0:T(8,128)S(1)}, f32[2,2,256,256]{3,2,1,0:T(8,128)}, u32[]{:S(2)}, u32[]{:S(2)}) collective-permute-start(f32[2,2,256,256]{3,2,1,0:T(8,128)S(1)} %get-tuple-element.8), channel_id=1, source_target_pairs={{0,8},{8,0},{16,24},{24,16},{32,40},{40,32},{48,56},{56,48},{64,72... | collective-permute-start | bytes 3145736 | tf_op jit(solution)/shard_map/ppermute | solution.py:19
  661.1 41.6 %all-to-all-start = ((f32[1,2,256,256]{3,1,0,2:T(2,128)}), f32[1,2,256,256]{3,1,0,2:T(2,128)S(1)}, u32[]{:S(2)}, u32[]{:S(2)}) async-start(f32[1,2,256,256]{3,1,0,2:T(2,128)} %copy.46), calls=%async_computation | async-start | bytes 1048576 | tf_op jit(solution)/shard_map/all_to_all | solution.py:113
  702.7 37.1 %all-to-all-start.1 = ((f32[1,2,256,256]{3,1,0,2:T(2,128)}), f32[1,2,256,256]{3,1,0,2:T(2,128)S(1)}, u32[]{:S(2)}, u32[]{:S(2)}) async-start(f32[1,2,256,256]{3,1,0,2:T(2,128)} %copy.49), calls=%async_computation.1 | async-start | bytes 1048576 | tf_op jit(solution)/shard_map/all_to_all | solution.py:120
  742.3 5.8 copy-start.7
  742.3 27.1 %all-to-all-start.2 = ((f32[64,4,256]{2,1,0:T(4,128)}), f32[64,4,256]{2,1,0:T(4,128)S(1)}, u32[]{:S(2)}, u32[]{:S(2)}) async-start(f32[64,4,256]{2,1,0:T(4,128)} %copy.54), calls=%async_computation.2 | async-start | bytes 524288 | tf_op jit(solution)/shard_map/all_to_all | solution.py:146
  748.1 4.8 collective-permute-start
  769.5 0.7 copy-start.8
where the time goes:
time: 772 us; the launch traced here: 771 us
  waiting for transfers between devices  629 us (81%)
  starting transfers between devices  88.6 us (11%)
  other arithmetic  19.8 us (3%)
  matrix products  18.9 us (2%)
  local copies, waits for them, and re-layouts  13 us (2%)
    ppermute x12, waiting for transfers between devices, from_partner(): return lax.ppermute(block, axis, route)  554 us
    ppermute x12, starting transfers between devices, from_partner(): return lax.ppermute(block, axis, route)  56 us
    all_to_all x1, waiting for transfers between devices, inverse_blocks(): lax.all_to_all(val_imag.reshape(1, 2, row_count, channels), 'seq', split_...  30.6 us
    all_to_all x1, waiting for transfers between devices, inverse_blocks(): lax.all_to_all(val_real.reshape(1, 2, row_count, channels), 'seq', split_...  26.7 us
    dot_general x8, matrix products, product(): return jnp.einsum(form, left, right, precision=exact_mode)  17.7 us
    all_to_all x1, waiting for transfers between devices, inverse_blocks(): lax.all_to_all(blocks, 'seq', split_axis=0, concat_axis=1, tiled=True)  16.5 us
  transfers between devices with their start and end apart: 18, of which 16 were waited for; matrix products, arithmetic and copies ran while one was open for 1% of the time, Pallas kernels for 0%

commit v1 on v0

v1 whole, which is shorter than its diff:
```python
import jax
import jax.numpy as jnp
import numpy as np
from jax import lax
from jax.experimental import pallas as pl
from jax.experimental.pallas import tpu as pltpu
from jax.sharding import PartitionSpec as P

f32 = jnp.float32
bf16 = jnp.bfloat16

BLOCKS = 64
ROWS = 256
OWN = 4
TOTAL = BLOCKS * ROWS
TAPS = 7


def halves(table):
    high = table.astype(jnp.bfloat16)
    low = (table - high.astype(np.float64)).astype(jnp.bfloat16)
    return high, low


def make_tables():
    turn = 2.0 * np.pi
    freq = np.arange(BLOCKS) + 0.25
    block = np.arange(BLOCKS)
    row = np.arange(ROWS)
    angle = turn * freq[:, None] * block[None, :] / BLOCKS
    high, low = halves(np.concatenate([np.cos(angle), -np.sin(angle)], axis=0))
    outer = np.concatenate([high, low, high], axis=1)
    high, low = halves(np.concatenate([np.cos(angle.T), -np.sin(angle.T)], axis=1) / TOTAL)
    outer_back = np.concatenate([high, low, high], axis=1)
    angle = turn * freq[:, None] * row[None, :] / TOTAL
    twist = np.stack([np.cos(angle), -np.sin(angle)]).astype(np.float32)
    angle = turn * (row[:, None] * row[None, :] % ROWS) / ROWS
    inner = np.stack(halves(np.concatenate([np.cos(angle), np.sin(angle)], axis=1)))
    return outer, outer_back, twist, inner


def split(value):
    high = value.astype(bf16)
    return high, (value - high.astype(f32)).astype(bf16)


def dot(left, right):
    return jnp.dot(left, right, preferred_element_type=f32)


def pack_kernel(key_ref, value_ref, long_ref, out_ref, stage_ref):
    long_t = long_ref[...].T
    long_high = long_t.astype(bf16).astype(f32)
    parts = (key_ref[...].astype(f32).T, value_ref[...].astype(f32).T, long_high, long_t - long_high)
    for place, part in enumerate(parts):
        for own in range(OWN):
            stage_ref[:, place * OWN + own, :] = part[own * BLOCKS : (own + 1) * BLOCKS]
    out_ref[...] = stage_ref[...].astype(bf16)


def filter_kernel(
    got_ref, taps_ref, gain_ref, outer_ref, back_ref, twist_ref, inner_ref, out_ref, stage_ref
):
    stage_ref[...] = got_ref[...].astype(f32)
    lane = lax.broadcasted_iota(jnp.int32, (BLOCKS, ROWS), 1)
    first = lax.broadcasted_iota(jnp.int32, (BLOCKS, ROWS), 0) == 0

    def short(value, branch, own):
        before = jnp.where(first, 0.0, pltpu.roll(value, 1, 0))
        total = taps_ref[branch, TAPS - 1, own] * value
        for back in range(1, TAPS):
            moved = pltpu.roll(jnp.where(lane >= ROWS - back, before, value), back, 1)
            total = total + taps_ref[branch, TAPS - 1 - back, own] * moved
        return total

    gated = []
    for own in range(OWN):
        key_mix = short(stage_ref[:, own, :], 0, own)
        value_mix = short(stage_ref[:, OWN + own, :], 1, own)
        gated.append(key_mix * value_mix)
    signal_high, signal_low = split(jnp.concatenate(gated, axis=1))
    long_high = jnp.concatenate(
        [stage_ref[:, 2 * OWN + own, :] for own in range(OWN)], axis=1
    ).astype(bf16)
    long_low = jnp.concatenate(
        [stage_ref[:, 3 * OWN + own, :] for own in range(OWN)], axis=1
    ).astype(bf16)
    twist_real = twist_ref[0]
    twist_imag = twist_ref[1]
    inner_high = inner_ref[0]
    inner_low = inner_ref[1]

    def inner_product(value):
        high, low = split(value)
        return dot(high, inner_high) + dot(high, inner_low) + dot(low, inner_high)

    def spectrum(high, low):
        across = dot(outer_ref[...], jnp.concatenate([high, high, low], axis=0))
        real = []
        imag = []
        for own in range(OWN):
            piece_real = across[:BLOCKS, own * ROWS : (own + 1) * ROWS]
            piece_imag = across[BLOCKS:, own * ROWS : (own + 1) * ROWS]
            real.append(piece_real * twist_real - piece_imag * twist_imag)
            imag.append(piece_real * twist_imag + piece_imag * twist_real)
        both = inner_product(jnp.concatenate(real + imag, axis=0))
        half = OWN * BLOCKS
        return (
            both[:half, :ROWS] + both[half:, ROWS:],
            both[half:, :ROWS] - both[:half, ROWS:],
        )

    signal_real, signal_imag = spectrum(signal_high, signal_low)
    long_real, long_imag = spectrum(long_high, long_low)
    prod_real = signal_real * long_real - signal_imag * long_imag
    prod_imag = signal_real * long_imag + signal_imag * long_real
    both = inner_product(jnp.concatenate([prod_real, prod_imag], axis=0))
    half = OWN * BLOCKS
    time_real = both[:half, :ROWS] - both[half:, ROWS:]
    time_imag = both[half:, :ROWS] + both[:half, ROWS:]
    real = []
    imag = []
    for own in range(OWN):
        piece_real = time_real[own * BLOCKS : (own + 1) * BLOCKS]
        piece_imag = time_imag[own * BLOCKS : (own + 1) * BLOCKS]
        real.append(piece_real * twist_real + piece_imag * twist_imag)
        imag.append(piece_imag * twist_real - piece_real * twist_imag)
    high, low = split(
        jnp.concatenate([jnp.concatenate(real, axis=1), jnp.concatenate(imag, axis=1)], axis=0)
    )
    mixed = dot(back_ref[...], jnp.concatenate([high, high, low], axis=0))
    for own in range(OWN):
        total = mixed[:, own * ROWS : (own + 1) * ROWS] + gain_ref[own] * gated[own]
        out_ref[:, 2 * own, :] = total[:, : ROWS // 2]
        out_ref[:, 2 * own + 1, :] = total[:, ROWS // 2 :]


def finish_kernel(got_ref, query_ref, out_ref):
    rows = []
    for own in range(OWN):
        rows.append(jnp.concatenate([got_ref[:, 2 * own, :], got_ref[:, 2 * own + 1, :]], axis=1))
    out_ref[...] = (query_ref[...] * jnp.concatenate(rows, axis=0).T).astype(bf16)


def in_vmem(count):
    return [pl.BlockSpec(memory_space=pltpu.VMEM)] * count


def short_filter(values, rim_part, weights):
    row_count = values.shape[0]
    padded = jnp.concatenate([rim_part, values], axis=0).astype(f32)
    total = weights[0] * padded[:row_count]
    for offset in range(1, weights.shape[0]):
        total = total + weights[offset] * padded[offset : offset + row_count]
    return total


def shards(query_branch, key_branch, value_branch, short_taps, long_taps, skip_gain):
    outer, outer_back, twist, inner = make_tables()
    packed = pl.pallas_call(
        pack_kernel,
        out_shape=jax.ShapeDtypeStruct((BLOCKS, 4 * OWN, ROWS), bf16),
        in_specs=in_vmem(3),
        out_specs=in_vmem(1)[0],
        scratch_shapes=[pltpu.VMEM((BLOCKS, 4 * OWN, ROWS), f32)],
        name="pack",
    )(key_branch, value_branch, long_taps)
    got = lax.all_to_all(packed, "seq", split_axis=0, concat_axis=0, tiled=True)
    place = lax.axis_index("seq")
    own_taps = lax.dynamic_index_in_dim(
        short_taps[1:].reshape(2, TAPS, OWN, BLOCKS), place, 3, keepdims=False
    )
    own_gain = lax.dynamic_index_in_dim(skip_gain.reshape(OWN, BLOCKS), place, 1, keepdims=False)
    mixed = pl.pallas_call(
        filter_kernel,
        out_shape=jax.ShapeDtypeStruct((BLOCKS, 2 * OWN, ROWS // 2), f32),
        in_specs=in_vmem(1) + [pl.BlockSpec(memory_space=pltpu.SMEM)] * 2 + in_vmem(4),
        out_specs=in_vmem(1)[0],
        scratch_shapes=[pltpu.VMEM((BLOCKS, 4 * OWN, ROWS), f32)],
        name="filter",
    )(got, own_taps, own_gain, outer, outer_back, twist, inner)
    back = lax.all_to_all(mixed, "seq", split_axis=0, concat_axis=0, tiled=True)
    rim = lax.ppermute(
        query_branch[-(TAPS - 1) :], "seq", [(i, i + 1) for i in range(BLOCKS - 1)]
    )
    query_mix = short_filter(query_branch, rim, short_taps[0])
    return pl.pallas_call(
        finish_kernel,
        out_shape=jax.ShapeDtypeStruct(query_branch.shape, bf16),
        in_specs=in_vmem(2),
        out_specs=in_vmem(1)[0],
        name="finish",
    )(back, query_mix)


def solution(mesh):
    return jax.shard_map(
        shards,
        mesh=mesh,
        in_specs=(
            P("seq", "ch"),
            P("seq", "ch"),
            P("seq", "ch"),
            P(None, None, "ch"),
            P("seq", "ch"),
            P("ch"),
        ),
        out_specs=P("seq", "ch"),
        check_vma=False,
    )
```

time: 772 us -> 91.5 us (0.12)
  waiting for transfers between devices: 629 us -> 47.7 us
  starting transfers between devices: 88.6 us -> 28.2 us
  matrix products: 18.9 us -> 0 us
  other arithmetic: 19.8 us -> 0.96 us
  Pallas kernels: 0 us -> 10.1 us
  local copies, waits for them, and re-layouts: 13 us -> 4.04 us
    ppermute x15 -> x1, waiting for transfers between devices: 556 us -> 1.28 us  [shards(): lax.ppermute(query_branch[-(TAPS - 1):], 'seq', [(i, i + 1) for i in rang...]
    ppermute x15 -> x1, starting transfers between devices: 66.4 us -> 3.47 us  [shards(): lax.ppermute(query_branch[-(TAPS - 1):], 'seq', [(i, i + 1) for i in rang...]
    all_to_all x3 -> x2, waiting for transfers between devices: 73.8 us -> 46.4 us  [the longest x1 30.3 us: shards(): got = lax.all_to_all(packed, 'seq', split_axis=0, concat_axis=0, tiled=True)]
    dot_general x10 -> x0, matrix products: 18.9 us -> none  [the longest x8 17.7 us: product(): return jnp.einsum(form, left, right, precision=exact_mode)]
    select_n x6 -> x0, other arithmetic: 15.3 us -> none  [forward_pairs(): cur_real = jnp.where(upper_side, high_real, cur_real + other_real)]
    pallas_call x0 -> x3, Pallas kernels: none -> 10.1 us  [the longest x1 5.76 us: shards(): pl.pallas_call(filter_kernel, out_shape=jax.ShapeDtypeStruct((BLOCKS, 2 *...]
    all_to_all x3 -> x2, starting transfers between devices: 22.2 us -> 24.7 us  [the longest x1 18.7 us: shards(): got = lax.all_to_all(packed, 'seq', split_axis=0, concat_axis=0, tiled=True)]
  transfers between devices with their start and end apart: 18 -> 3, of which waited for: 16 -> 3; matrix products, arithmetic and copies ran while one was open for 1% -> 3% of each run, Pallas kernels for 0% -> 0%
where the time goes in v1:
time: 91.5 us; the launch traced here: 91.1 us
  waiting for transfers between devices  47.7 us (52%)
  starting transfers between devices  28.2 us (31%)
  Pallas kernels  10.1 us (11%)
  local copies, waits for them, and re-layouts  4.04 us (4%)
  other arithmetic  0.96 us (1%)
    all_to_all x1, waiting for transfers between devices, shards(): got = lax.all_to_all(packed, 'seq', split_axis=0, concat_axis=0, tiled=True)  30.3 us
    all_to_all x1, starting transfers between devices, shards(): got = lax.all_to_all(packed, 'seq', split_axis=0, concat_axis=0, tiled=True)  18.7 us
    all_to_all x1, waiting for transfers between devices, shards(): back = lax.all_to_all(mixed, 'seq', split_axis=0, concat_axis=0, tiled=True)  16.1 us
    all_to_all x1, starting transfers between devices, shards(): back = lax.all_to_all(mixed, 'seq', split_axis=0, concat_axis=0, tiled=True)  5.96 us
    pallas_call x1, Pallas kernels, shards(): pl.pallas_call(filter_kernel, out_shape=jax.ShapeDtypeStruct((BLOCKS, 2 *...  5.76 us
    ppermute x1, starting transfers between devices, shards(): lax.ppermute(query_branch[-(TAPS - 1):], 'seq', [(i, i + 1) for i in rang...  3.47 us
    pallas_call x1, Pallas kernels, shards(): pl.pallas_call(pack_kernel, out_shape=jax.ShapeDtypeStruct((BLOCKS, 4 * O...  2.47 us
    pallas_call x1, Pallas kernels, shards(): pl.pallas_call(finish_kernel, out_shape=jax.ShapeDtypeStruct(query_branch...  1.89 us
  transfers between devices with their start and end apart: 3, of which 3 were waited for; matrix products, arithmetic and copies ran while one was open for 3% of the time, Pallas kernels for 0%

profile of v1, /device:TPU:6, one launch (start us, length us, event | category | flops | bytes accessed | tf_op | source)
XLA Modules:
  0.0 91.1 jit_solution(3909772390095987762)
XLA Ops:
  0.0 2.5 %pack.1 = bf16[64,16,256]{2,1,0:T(8,128)(2,1)} custom-call(bf16[256,256]{1,0:T(8,128)(2,1)} %key_ref.1, bf16[256,256]{1,0:T(8,128)(2,1)} %value_ref.1, f32[256,256]{1,0:T(8,128)} %long_ref.1), custom_call_target="tpu_custom_call" | custom-call | tf_op jit(solution)/shard_map/pack/pallas_call | solution.py:160
  2.5 18.7 %all-to-all-start = ((bf16[64,16,256]{2,1,0:T(8,128)(2,1)}), bf16[64,16,256]{2,1,0:T(8,128)(2,1)S(1)}, u32[]{:S(2)}, u32[]{:S(2)}) async-start(bf16[64,16,256]{2,1,0:T(8,128)(2,1)} %pack.1), calls=%async_computation | async-start | bytes 1048576 | tf_op jit(solution)/shard_map/all_to_all | solution.py:168
  21.2 0.0 slice-start
  21.2 0.7 slice-done
  21.9 0.1 reshape.20
  22.0 0.1 constant_dynamic-slice_fusion
  22.1 0.1 copy.17
  22.2 0.0 copy-start.4
  22.2 0.7 copy.16.taps_ref
  22.9 0.0 copy-done.4
  22.9 0.1 reshape.21
  23.0 0.7 dynamic-slice_reduce_fusion.gain_ref
  23.7 30.3 %all-to-all-done.got_ref = bf16[64,16,256]{2,1,0:T(8,128)(2,1)S(1)} async-done(((bf16[64,16,256]{2,1,0:T(8,128)(2,1)}), bf16[64,16,256]{2,1,0:T(8,128)(2,1)S(1)}, u32[]{:S(2)}, u32[]{:S(2)}) %all-to-all-start) | async-done | bytes 524320 | tf_op jit(solution)/shard_map/all_to_all | solution.py:168
  54.0 0.0 copy-start
  54.0 0.8 copy-done
  54.8 5.8 %filter.1 = f32[64,8,128]{2,1,0:T(8,128)} custom-call(bf16[64,16,256]{2,1,0:T(8,128)(2,1)} %copy-done, f32[2,7,4]{2,1,0:T(8,128)} %copy.16.taps_ref, f32[4]{0:T(128)} %dynamic-slice_reduce_fusion.gain_ref, bf16[128,192]{1,0:T(8,128)(2,1)} %constant.24.clone.outer_ref, bf16[64,384]{1,0:T(8,128)(2,1)} %constant.25.clone.back_ref, ...), custom_call_target="tpu_custom_call" | custom-call | tf_op jit(solution)/shard_map/filter/pallas_call | solution.py:174
  60.6 0.0 copy-start.2
  60.6 0.0 copy-start.3
  60.6 6.0 %all-to-all-start.1 = ((f32[64,8,128]{2,1,0:T(8,128)}), f32[64,8,128]{2,1,0:T(8,128)S(1)}, u32[]{:S(2)}, u32[]{:S(2)}) async-start(f32[64,8,128]{2,1,0:T(8,128)} %filter.1), calls=%async_computation.1 | async-start | bytes 524288 | tf_op jit(solution)/shard_map/all_to_all | solution.py:182
  66.6 0.0 copy-done.2
  66.6 3.5 %collective-permute-start = (bf16[6,256]{1,0:T(8,128)(2,1)S(1)}, bf16[6,256]{1,0:T(8,128)(2,1)S(1)}, u32[]{:S(2)}, u32[]{:S(2)}) collective-permute-start(bf16[6,256]{1,0:T(8,128)(2,1)S(1)} %slice.65), channel_id=1, source_target_pairs={{0,8},{8,16},{16,24},{24,32},{32,40},{40,48},{48,56},{56,64},{64,7... | collective-permute-start | bytes 9224 | tf_op jit(solution)/shard_map/ppermute | solution.py:183
  70.1 0.0 copy-done.3
  70.1 1.3 %collective-permute-done = bf16[6,256]{1,0:T(8,128)(2,1)S(1)} collective-permute-done((bf16[6,256]{1,0:T(8,128)(2,1)S(1)}, bf16[6,256]{1,0:T(8,128)(2,1)S(1)}, u32[]{:S(2)}, u32[]{:S(2)}) %collective-permute-start) | collective-permute-done | bytes 3104 | tf_op jit(solution)/shard_map/ppermute | solution.py:183
  71.4 0.9 %fusion.query_ref = f32[256,256]{1,0:T(8,128)} fusion(f32[262,256]{1,0:T(8,128)S(1)} %maximum_convert_fusion, f32[256]{0:T(256)S(1)} %bitcast.14, f32[256]{0:T(256)S(1)} %bitcast.15, f32[256]{0:T(256)S(1)} %bitcast.10, f32[256]{0:T(256)S(1)} %bitcast.11, f32[256]{0:T(256)S(1)} %bitcast.12, f32[256]{0:T(256)S(1)} %bitcast.13, f32[256]{0:T(256)S(1)} %bitcast.9), kind=kLoop, calls=%fused_computation.1 | loop fusion | flops 851968 | bytes 2104320 | tf_op jit(solution)/shard_map/add | solution.py:154
  72.3 16.1 %all-to-all-done.1.got_ref = f32[64,8,128]{2,1,0:T(8,128)S(1)} async-done(((f32[64,8,128]{2,1,0:T(8,128)}), f32[64,8,128]{2,1,0:T(8,128)S(1)}, u32[]{:S(2)}, u32[]{:S(2)}) %all-to-all-start.1) | async-done | bytes 262176 | tf_op jit(solution)/shard_map/all_to_all | solution.py:182
  88.5 0.0 copy-start.1
  88.5 0.7 copy-done.1
  89.2 1.9 %finish.1 = bf16[256,256]{1,0:T(8,128)(2,1)} custom-call(f32[64,8,128]{2,1,0:T(8,128)} %copy-done.1, f32[256,256]{1,0:T(8,128)} %fusion.query_ref), custom_call_target="tpu_custom_call" | custom-call | tf_op jit(solution)/shard_map/finish/pallas_call | solution.py:187
  (3 shorter events, 0.0 us)
Async XLA Ops:
  2.5 51.6 %all-to-all-start = ((bf16[64,16,256]{2,1,0:T(8,128)(2,1)}), bf16[64,16,256]{2,1,0:T(8,128)(2,1)S(1)}, u32[]{:S(2)}, u32[]{:S(2)}) async-start(bf16[64,16,256]{2,1,0:T(8,128)(2,1)} %pack.1), calls=%async_computation | async-start | bytes 1048576 | tf_op jit(solution)/shard_map/all_to_all | solution.py:168
  21.2 0.7 slice-start
  22.2 0.7 copy-start.4
  54.0 0.8 copy-start
  60.6 6.0 %copy-start.2 = (bf16[256,256]{1,0:T(8,128)(2,1)S(1)}, bf16[256,256]{1,0:T(8,128)(2,1)}, u32[]{:S(2)}) copy-start(bf16[256,256]{1,0:T(8,128)(2,1)} %param.10) | copy-start | bytes 393220
  60.6 9.5 %copy-start.3 = (f32[3,7,256]{2,1,0:T(8,128)S(1)}, f32[3,7,256]{2,1,0:T(8,128)}, u32[]{:S(2)}) copy-start(f32[3,7,256]{2,1,0:T(8,128)} %param.13) | copy-start | bytes 64516
  60.6 27.9 %all-to-all-start.1 = ((f32[64,8,128]{2,1,0:T(8,128)}), f32[64,8,128]{2,1,0:T(8,128)S(1)}, u32[]{:S(2)}, u32[]{:S(2)}) async-start(f32[64,8,128]{2,1,0:T(8,128)} %filter.1), calls=%async_computation.1 | async-start | bytes 524288 | tf_op jit(solution)/shard_map/all_to_all | solution.py:182
  66.6 4.8 %collective-permute-start = (bf16[6,256]{1,0:T(8,128)(2,1)S(1)}, bf16[6,256]{1,0:T(8,128)(2,1)S(1)}, u32[]{:S(2)}, u32[]{:S(2)}) collective-permute-start(bf16[6,256]{1,0:T(8,128)(2,1)S(1)} %slice.65), channel_id=1, source_target_pairs={{0,8},{8,16},{16,24},{24,32},{32,40},{40,48},{48,56},{56,64},{64,7... | collective-permute-start | bytes 9224 | tf_op jit(solution)/shard_map/ppermute | solution.py:183
  88.5 0.7 copy-start.1

commit v2 on v1

v2 whole, which is shorter than its diff:
```python
import jax
import jax.numpy as jnp
import numpy as np
from jax import lax
from jax.experimental import pallas as pl
from jax.experimental.pallas import tpu as pltpu
from jax.sharding import PartitionSpec as P

f32 = jnp.float32
bf16 = jnp.bfloat16

BLOCKS = 64
ROWS = 256
OWN = 4
TOTAL = BLOCKS * ROWS
TAPS = 7
LANES = ROWS // 2
SENT = 6 * OWN
BACK = 2 * OWN
HOLD = 7000
SIDE_LEN = 8
LEAD = 42
LEAD_BACK = 34
TURN = (LEAD_BACK - LEAD) // SIDE_LEN % SIDE_LEN


def order(lead):
    place = [rank % SIDE_LEN * SIDE_LEN + rank // SIDE_LEN for rank in range(BLOCKS)]
    return [(at + lead) % BLOCKS for at in place]


START_GROUP = -LEAD % SIDE_LEN
START_ROW = -LEAD % BLOCKS // SIDE_LEN

FLOOR = 2.0**-10
CODE_LOW = -125.0
CODE_RATE = 250.0 / np.log2(1.0 + 1.6 / FLOOR)


def halves(table):
    high = table.astype(jnp.bfloat16)
    low = (table - high.astype(np.float64)).astype(jnp.bfloat16)
    return high, low


def make_tables():
    turn = 2.0 * np.pi
    freq = np.arange(BLOCKS) + 0.25
    row = np.arange(ROWS)
    angle = turn * freq[:, None] * np.array(order(LEAD))[None, :] / BLOCKS
    high, low = halves(np.concatenate([np.cos(angle), -np.sin(angle)], axis=0))
    outer = np.concatenate([high, low, high], axis=1)
    angle = turn * freq[:, None] * np.array(order(LEAD_BACK))[None, :] / BLOCKS
    high, low = halves(np.concatenate([np.cos(angle.T), -np.sin(angle.T)], axis=1) / TOTAL)
    outer_back = np.concatenate([high, low, high], axis=1)
    angle = turn * freq[:, None] * row[None, :] / TOTAL
    twist = np.stack([np.cos(angle), -np.sin(angle)]).astype(np.float32)
    angle = turn * (row[:, None] * row[None, :] % ROWS) / ROWS
    inner = np.stack(halves(np.concatenate([np.cos(angle), np.sin(angle)], axis=1)))
    return outer, outer_back, twist, inner


def split(value):
    high = value.astype(bf16)
    return high, (value - high.astype(f32)).astype(bf16)


def turned(value, shift):
    groups = value.reshape(BLOCKS // SIDE_LEN, SIDE_LEN, LANES)
    return pltpu.roll(groups, shift % SIDE_LEN, 1).reshape(BLOCKS, LANES)


def dot(left, right):
    return jnp.dot(left, right, preferred_element_type=f32)


def encode(value):
    code = jnp.exp2(CODE_RATE * jnp.log2(1.0 + jnp.abs(value) * (1.0 / FLOOR)) + CODE_LOW)
    return jnp.where(value < 0.0, -code, code)


def decode(code):
    size = (jnp.exp2((jnp.log2(jnp.abs(code)) - CODE_LOW) * (1.0 / CODE_RATE)) - 1.0) * FLOOR
    return jnp.where(code < 0.0, -size, size)


def pack_kernel(hold_ref, key_ref, value_ref, long_ref, out_ref, stage_ref):
    parts = (
        key_ref[...].astype(f32).T,
        value_ref[...].astype(f32).T,
        encode(long_ref[...]).T,
    )
    for place, part in enumerate(parts):
        for own in range(OWN):
            piece = part[own * BLOCKS : (own + 1) * BLOCKS]
            row = 2 * (place * OWN + own)
            stage_ref[pl.ds(row, BLOCKS, stride=SENT), :] = piece[:, :LANES]
            stage_ref[pl.ds(row + 1, BLOCKS, stride=SENT), :] = piece[:, LANES:]
    out_ref[...] = stage_ref[...].astype(bf16)
    pl.delay(hold_ref[0])


def filter_kernel(
    got_ref, taps_ref, gain_ref, outer_ref, back_ref, twist_ref, inner_ref, out_ref, stage_ref
):
    stage_ref[...] = got_ref[...].astype(f32)
    twist_real = twist_ref[0]
    twist_imag = twist_ref[1]
    inner_high = inner_ref[0]
    inner_low = inner_ref[1]
    half = OWN * BLOCKS

    def staged(row):
        return stage_ref[pl.ds(row, BLOCKS, stride=SENT), :]

    def inner_product(value):
        high, low = split(value)
        return dot(high, inner_high) + dot(high, inner_low) + dot(low, inner_high)

    def spectrum(signal):
        high, low = split(signal)
        across = dot(outer_ref[...], jnp.concatenate([high, high, low], axis=0))
        real = []
        imag = []
        for own in range(OWN):
            piece_real = across[:BLOCKS, own * ROWS : (own + 1) * ROWS]
            piece_imag = across[BLOCKS:, own * ROWS : (own + 1) * ROWS]
            real.append(piece_real * twist_real - piece_imag * twist_imag)
            imag.append(piece_real * twist_imag + piece_imag * twist_real)
        both = inner_product(jnp.concatenate(real + imag, axis=0))
        return (
            both[:half, :ROWS] + both[half:, ROWS:],
            both[half:, :ROWS] - both[:half, ROWS:],
        )

    first_row = 4 * OWN
    long_real, long_imag = spectrum(
        decode(jnp.concatenate([staged(first_row + i) for i in range(2 * OWN)], axis=1))
    )

    lane = lax.broadcasted_iota(jnp.int32, (BLOCKS, LANES), 1)
    first = lax.broadcasted_iota(jnp.int32, (SIDE_LEN, LANES), 0) == START_ROW

    def short(branch, own):
        early = staged(2 * (branch * OWN + own))
        late = staged(2 * (branch * OWN + own) + 1)
        groups = [pltpu.roll(late[-SIDE_LEN:], 1, 0)]
        groups += [late[i : i + SIDE_LEN] for i in range(0, BLOCKS - SIDE_LEN, SIDE_LEN)]
        groups[START_GROUP] = jnp.where(first, 0.0, groups[START_GROUP])
        tap = taps_ref[branch, TAPS - 1, own]
        early_sum = tap * early
        late_sum = tap * late
        for back in range(1, TAPS):
            tap = taps_ref[branch, TAPS - 1 - back, own]
            moved_early = pltpu.roll(early, back, 1)
            moved_late = pltpu.roll(late, back, 1)
            moved_before = [
                pltpu.roll(group, back, 1)
                if i in (0, START_GROUP)
                else moved_late[(i - 1) * SIDE_LEN : i * SIDE_LEN]
                for i, group in enumerate(groups)
            ]
            moved_before = jnp.concatenate(moved_before, axis=0)
            early_sum = early_sum + tap * jnp.where(lane < back, moved_before, moved_early)
            late_sum = late_sum + tap * jnp.where(lane < back, moved_early, moved_late)
        return early_sum, late_sum

    gated = []
    for own in range(OWN):
        for key_mix, value_mix in zip(short(0, own), short(1, own)):
            gated.append(key_mix * value_mix)
    signal_real, signal_imag = spectrum(jnp.concatenate(gated, axis=1))
    prod_real = signal_real * long_real - signal_imag * long_imag
    prod_imag = signal_real * long_imag + signal_imag * long_real
    both = inner_product(jnp.concatenate([prod_real, prod_imag], axis=0))
    time_real = both[:half, :ROWS] - both[half:, ROWS:]
    time_imag = both[half:, :ROWS] + both[:half, ROWS:]
    real = []
    imag = []
    for own in range(OWN):
        piece_real = time_real[own * BLOCKS : (own + 1) * BLOCKS]
        piece_imag = time_imag[own * BLOCKS : (own + 1) * BLOCKS]
        real.append(piece_real * twist_real + piece_imag * twist_imag)
        imag.append(piece_imag * twist_real - piece_real * twist_imag)
    high, low = split(
        jnp.concatenate([jnp.concatenate(real, axis=1), jnp.concatenate(imag, axis=1)], axis=0)
    )
    mixed = dot(back_ref[...], jnp.concatenate([high, high, low], axis=0))
    for i in range(2 * OWN):
        out_ref[pl.ds(i, BLOCKS, stride=BACK), :] = (
            mixed[:, i * LANES : (i + 1) * LANES] + gain_ref[i // 2] * turned(gated[i], -TURN)
        )


def finish_kernel(got_ref, query_ref, out_ref):
    rows = []
    for own in range(OWN):
        early = got_ref[pl.ds(2 * own, BLOCKS, stride=BACK), :]
        late = got_ref[pl.ds(2 * own + 1, BLOCKS, stride=BACK), :]
        rows.append(jnp.concatenate([turned(early, TURN), turned(late, TURN)], axis=1))
    out_ref[...] = (query_ref[...] * jnp.concatenate(rows, axis=0).T).astype(bf16)


def in_vmem(count):
    return [pl.BlockSpec(memory_space=pltpu.VMEM)] * count


def short_filter(values, rim_part, weights):
    row_count = values.shape[0]
    padded = jnp.concatenate([rim_part, values], axis=0).astype(f32)
    total = weights[0] * padded[:row_count]
    for offset in range(1, weights.shape[0]):
        total = total + weights[offset] * padded[offset : offset + row_count]
    return total


def near(value):
    return pltpu.with_memory_space_constraint(value, pltpu.VMEM)


def exchange(blocks, lead):
    moved = lax.all_to_all(
        blocks.reshape(BLOCKS, -1, LANES),
        "seq",
        split_axis=0,
        concat_axis=0,
        axis_index_groups=[order(lead)],
        tiled=True,
    )
    return moved.reshape(blocks.shape)


def shards(query_branch, key_branch, value_branch, short_taps, long_taps, skip_gain):
    outer, outer_back, twist, inner = make_tables()
    rim = lax.ppermute(
        query_branch[-(TAPS - 1) :], "seq", [(i, i + 1) for i in range(BLOCKS - 1)]
    )
    query_mix = short_filter(query_branch, rim, short_taps[0])
    hold = jnp.full((1,), HOLD * (1 - lax.axis_index("ch") % 2), jnp.int32)
    packed = pl.pallas_call(
        pack_kernel,
        out_shape=pltpu.VMEM((BLOCKS * SENT, LANES), bf16),
        in_specs=[pl.BlockSpec(memory_space=pltpu.SMEM)] + in_vmem(3),
        out_specs=in_vmem(1)[0],
        scratch_shapes=[pltpu.VMEM((BLOCKS * SENT, LANES), f32)],
        name="pack",
    )(hold, key_branch, value_branch, long_taps)
    got = exchange(packed, LEAD)
    got, query_mix = lax.optimization_barrier((got, query_mix))
    place = (lax.axis_index("seq") + BLOCKS - LEAD) % BLOCKS
    place = place % SIDE_LEN * SIDE_LEN + place // SIDE_LEN
    own_taps = lax.dynamic_index_in_dim(
        short_taps[1:].reshape(2, TAPS, OWN, BLOCKS), place, 3, keepdims=False
    )
    own_gain = lax.dynamic_index_in_dim(skip_gain.reshape(OWN, BLOCKS), place, 1, keepdims=False)
    mixed = pl.pallas_call(
        filter_kernel,
        out_shape=pltpu.VMEM((BLOCKS * BACK, LANES), f32),
        in_specs=in_vmem(1) + [pl.BlockSpec(memory_space=pltpu.SMEM)] * 2 + in_vmem(4),
        out_specs=in_vmem(1)[0],
        scratch_shapes=[pltpu.VMEM((BLOCKS * SENT, LANES), f32)],
        name="filter",
    )(near(got), own_taps, own_gain, near(outer), near(outer_back), near(twist), near(inner))
    back = exchange(mixed, LEAD_BACK)
    return pl.pallas_call(
        finish_kernel,
        out_shape=jax.ShapeDtypeStruct(query_branch.shape, bf16),
        in_specs=in_vmem(2),
        out_specs=in_vmem(1)[0],
        name="finish",
    )(near(back), near(query_mix))


def solution(mesh):
    return jax.shard_map(
        shards,
        mesh=mesh,
        in_specs=(
            P("seq", "ch"),
            P("seq", "ch"),
            P("seq", "ch"),
            P(None, None, "ch"),
            P("seq", "ch"),
            P("ch"),
        ),
        out_specs=P("seq", "ch"),
        check_vma=False,
    )
```

time: 91.5 us -> 70.2 us (0.77)
  waiting for transfers between devices: 47.7 us -> 6.27 us
  blocking collectives: 0 us -> 22.6 us
  starting transfers between devices: 28.2 us -> 23.2 us
  Pallas kernels: 10.1 us -> 14 us
    all_to_all x2 -> x1, waiting for transfers between devices: 46.4 us -> 6.26 us  [exchange(): lax.all_to_all(blocks.reshape(BLOCKS, -1, LANES), 'seq', split_axis=0, co...]
    all_to_all x0 -> x1, blocking collectives: none -> 22.6 us  [exchange(): lax.all_to_all(blocks.reshape(BLOCKS, -1, LANES), 'seq', split_axis=0, co...]
    pallas_call x2, Pallas kernels: 8.23 us -> 13.2 us  [the longest x1 9.11 us: shards(): pl.pallas_call(pack_kernel, out_shape=pltpu.VMEM((BLOCKS * SENT, LANES),...]
    all_to_all x2 -> x1, starting transfers between devices: 24.7 us -> 21.3 us  [exchange(): lax.all_to_all(blocks.reshape(BLOCKS, -1, LANES), 'seq', split_axis=0, co...]
    ppermute x1, starting transfers between devices: 3.47 us -> 1.92 us  [shards(): lax.ppermute(query_branch[-(TAPS - 1):], 'seq', [(i, i + 1) for i in rang...]
    ppermute x1, waiting for transfers between devices: 1.28 us -> 0.01 us  [shards(): lax.ppermute(query_branch[-(TAPS - 1):], 'seq', [(i, i + 1) for i in rang...]
    pallas_call x1, Pallas kernels: 1.89 us -> 0.79 us  [shards(): pl.pallas_call(finish_kernel, out_shape=jax.ShapeDtypeStruct(query_branch...]
  transfers between devices with their start and end apart: 3 -> 2, of which waited for: 3 -> 1; matrix products, arithmetic and copies ran while one was open for 3% -> 3% of each run, Pallas kernels for 0% -> 0%
where the time goes in v2:
time: 70.2 us; the launch traced here: 69.7 us
  starting transfers between devices  23.2 us (33%)
  blocking collectives  22.6 us (32%)
  Pallas kernels  14 us (20%)
  waiting for transfers between devices  6.27 us (9%)
  local copies, waits for them, and re-layouts  3.22 us (5%)
    all_to_all x1, blocking collectives, exchange(): lax.all_to_all(blocks.reshape(BLOCKS, -1, LANES), 'seq', split_axis=0, co...  22.6 us
    all_to_all x1, starting transfers between devices, exchange(): lax.all_to_all(blocks.reshape(BLOCKS, -1, LANES), 'seq', split_axis=0, co...  21.3 us
    pallas_call x1, Pallas kernels, shards(): pl.pallas_call(pack_kernel, out_shape=pltpu.VMEM((BLOCKS * SENT, LANES),...  9.11 us
    all_to_all x1, waiting for transfers between devices, exchange(): lax.all_to_all(blocks.reshape(BLOCKS, -1, LANES), 'seq', split_axis=0, co...  6.26 us
    pallas_call x1, Pallas kernels, shards(): pl.pallas_call(filter_kernel, out_shape=pltpu.VMEM((BLOCKS * BACK, LANES)...  4.13 us
    ppermute x1, starting transfers between devices, shards(): lax.ppermute(query_branch[-(TAPS - 1):], 'seq', [(i, i + 1) for i in rang...  1.92 us
  transfers between devices with their start and end apart: 2, of which 1 were waited for; matrix products, arithmetic and copies ran while one was open for 3% of the time, Pallas kernels for 0%

profile of v2, /device:TPU:6, one launch (start us, length us, event | category | flops | bytes accessed | tf_op | source)
XLA Modules:
  0.0 69.7 jit_solution(14175744335198039767)
XLA Ops:
  0.0 9.1 %pack.1 = bf16[1536,128]{1,0:T(8,128)(2,1)} custom-call(s32[1]{0:T(128)} %bitcast.hold_ref, bf16[256,256]{1,0:T(8,128)(2,1)} %key_ref.1, bf16[256,256]{1,0:T(8,128)(2,1)} %value_ref.1, f32[256,256]{1,0:T(8,128)} %long_ref.1), custom_call_target="tpu_custom_call" | custom-call | tf_op jit(solution)/shard_map/pack/pallas_call | solution.py:240
  9.1 0.0 copy-start.4
  9.1 21.3 %all-to-all-start = ((bf16[64,24,128]{2,1,0:T(8,128)(2,1)}), bf16[64,24,128]{2,1,0:T(8,128)(2,1)S(1)}, u32[]{:S(2)}, u32[]{:S(2)}) async-start(bf16[64,24,128]{2,1,0:T(8,128)(2,1)} %bitcast.1), calls=%async_computation | async-start | bytes 786432 | tf_op jit(solution)/shard_map/all_to_all | solution.py:222
  30.4 0.0 copy-done.4
  30.4 1.9 %collective-permute-start = (bf16[6,256]{1,0:T(8,128)(2,1)S(1)}, bf16[6,256]{1,0:T(8,128)(2,1)S(1)}, u32[]{:S(2)}, u32[]{:S(2)}) collective-permute-start(bf16[6,256]{1,0:T(8,128)(2,1)S(1)} %slice.64), channel_id=1, source_target_pairs={{0,8},{8,16},{16,24},{24,32},{32,40},{40,48},{48,56},{56,64},{64,7... | collective-permute-start | bytes 9224 | tf_op jit(solution)/shard_map/ppermute | solution.py:235
  32.4 0.0 slice-start
  32.4 0.7 %slice-done = f32[2,7,256]{2,1,0:T(8,128)S(1)} async-done(((f32[3,7,256]{2,1,0:T(8,128)}), f32[2,7,256]{2,1,0:T(8,128)S(1)}, s32[]{:S(2)}) %slice-start) | async-done | bytes 14360 | tf_op jit(solution)/shard_map/slice | solution.py:253
  33.1 0.0 copy-start.5
  33.1 0.1 reshape.34
  33.2 0.7 copy-done.5
  33.9 0.1 constant_dynamic-slice_fusion
  34.0 0.1 copy.17
  34.1 0.0 copy-start.6
  34.1 0.7 %copy.16.taps_ref = f32[2,7,4]{2,1,0:T(8,128)} copy(f32[2,7,4]{1,2,0:T(4,128)S(1)} %bitcast.16) | data formatting | bytes 448 | tf_op jit(solution)/shard_map/jit(dynamic_index_in_dim)/squeeze | solution.py:252
  34.8 0.0 copy-done.6
  34.8 0.1 reshape.35
  34.9 0.7 %dynamic-slice_reduce_fusion.gain_ref = f32[4]{0:T(128)} fusion(f32[4,64]{1,0:T(4,128)S(1)} %reshape.35, s32[]{:T(128)S(6)} %select_n.29), kind=kLoop, calls=%fused_computation.14 | loop fusion | bytes 36 | tf_op jit(solution)/shard_map/jit(dynamic_index_in_dim)/dynamic_slice | solution.py:255
  35.6 0.0 collective-permute-done
  35.6 0.0 copy-start
  35.7 0.0 copy-start.1
  35.7 0.0 copy-start.2
  35.7 0.0 copy-start.3
  35.7 0.2 fusion.query_ref
  35.9 6.3 %all-to-all-done = bf16[64,24,128]{2,1,0:T(8,128)(2,1)S(1)} async-done(((bf16[64,24,128]{2,1,0:T(8,128)(2,1)}), bf16[64,24,128]{2,1,0:T(8,128)(2,1)S(1)}, u32[]{:S(2)}, u32[]{:S(2)}) %all-to-all-start) | async-done | bytes 393248 | tf_op jit(solution)/shard_map/all_to_all | solution.py:222
  42.2 0.0 copy-done
  42.2 0.0 copy-done.1
  42.2 0.0 copy-done.2
  42.2 0.0 copy-done.3
  42.2 4.1 %filter.1 = f32[512,128]{1,0:T(8,128)S(1)} custom-call(bf16[1536,128]{1,0:T(8,128)(2,1)S(1)} %bitcast.13, f32[2,7,4]{2,1,0:T(8,128)} %copy.16.taps_ref, f32[4]{0:T(128)} %dynamic-slice_reduce_fusion.gain_ref, bf16[128,192]{1,0:T(8,128)(2,1)S(1)} %copy-done.2, bf16[64,384]{1,0:T(8,128)(2,1)S(1)} %copy-done.3, f32[2,64,256]{2,1,0:T(8,128)S(1)} %copy-done.1, ...), custom_call_target="tpu_custom_call" | custom-call | tf_op jit(solution)/shard_map/filter/pallas_call | solution.py:256
  46.3 22.6 %all_to_all.10 = f32[64,8,128]{2,1,0:T(8,128)S(1)} all-to-all(f32[64,8,128]{2,1,0:T(8,128)S(1)} %bitcast.15), channel_id=1, replica_groups={{272,336,400,464,16,80,144,208,280,344,408,472,24,88,152,216,288,352,41..., dimensions={0} | all-to-all | bytes 524288 | tf_op jit(solution)/shard_map/all_to_all | solution.py:222
  68.9 0.8 %finish.1 = bf16[256,256]{1,0:T(8,128)(2,1)} custom-call(f32[512,128]{1,0:T(8,128)S(1)} %bitcast.14, f32[256,256]{1,0:T(8,128)S(1)} %fusion.query_ref), custom_call_target="tpu_custom_call" | custom-call | tf_op jit(solution)/shard_map/finish/pallas_call | solution.py:265
  (3 shorter events, 0.0 us)
Async XLA Ops:
  9.1 21.3 %copy-start.4 = (bf16[256,256]{1,0:T(8,128)(2,1)S(1)}, bf16[256,256]{1,0:T(8,128)(2,1)}, u32[]{:S(2)}) copy-start(bf16[256,256]{1,0:T(8,128)(2,1)} %param.10) | copy-start | bytes 393220
  9.1 33.1 %all-to-all-start = ((bf16[64,24,128]{2,1,0:T(8,128)(2,1)}), bf16[64,24,128]{2,1,0:T(8,128)(2,1)S(1)}, u32[]{:S(2)}, u32[]{:S(2)}) async-start(bf16[64,24,128]{2,1,0:T(8,128)(2,1)} %bitcast.1), calls=%async_computation | async-start | bytes 786432 | tf_op jit(solution)/shard_map/all_to_all | solution.py:222
  30.4 5.2 %collective-permute-start = (bf16[6,256]{1,0:T(8,128)(2,1)S(1)}, bf16[6,256]{1,0:T(8,128)(2,1)S(1)}, u32[]{:S(2)}, u32[]{:S(2)}) collective-permute-start(bf16[6,256]{1,0:T(8,128)(2,1)S(1)} %slice.64), channel_id=1, source_target_pairs={{0,8},{8,16},{16,24},{24,32},{32,40},{40,48},{48,56},{56,64},{64,7... | collective-permute-start | bytes 9224 | tf_op jit(solution)/shard_map/ppermute | solution.py:235
  32.4 0.7 %slice-start = ((f32[3,7,256]{2,1,0:T(8,128)}), f32[2,7,256]{2,1,0:T(8,128)S(1)}, s32[]{:S(2)}) async-start(f32[3,7,256]{2,1,0:T(8,128)} %param.13), calls=%async_computation.2 | async-start | bytes 32768 | tf_op jit(solution)/shard_map/slice | solution.py:253
  33.1 0.7 %copy-start.5 = (f32[3,7,256]{2,1,0:T(8,128)S(1)}, f32[3,7,256]{2,1,0:T(8,128)}, u32[]{:S(2)}) copy-start(f32[3,7,256]{2,1,0:T(8,128)} %param.13) | copy-start | bytes 64516
  34.1 0.7 %copy-start.6 = (f32[256]{0:T(256)S(1)}, f32[256]{0:T(256)}, u32[]{:S(2)}) copy-start(f32[256]{0:T(256)} %param.15) | copy-start | bytes 3076
  35.6 6.5 %copy-start = (bf16[2,256,512]{2,1,0:T(8,128)(2,1)S(1)}, bf16[2,256,512]{2,1,0:T(8,128)(2,1)}, u32[]{:S(2)}) copy-start(bf16[2,256,512]{2,1,0:T(8,128)(2,1)} %constant.80.clone.inner_ref) | copy-start | bytes 1572868
  35.7 6.5 %copy-start.1 = (f32[2,64,256]{2,1,0:T(8,128)S(1)}, f32[2,64,256]{2,1,0:T(8,128)}, u32[]{:S(2)}) copy-start(f32[2,64,256]{2,1,0:T(8,128)} %constant.79.clone.twist_ref) | copy-start | bytes 393220
  35.7 6.5 %copy-start.2 = (bf16[128,192]{1,0:T(8,128)(2,1)S(1)}, bf16[128,192]{1,0:T(8,128)(2,1)}, u32[]{:S(2)}) copy-start(bf16[128,192]{1,0:T(8,128)(2,1)} %constant.77.clone.outer_ref) | copy-start | bytes 147460
  35.7 6.5 %copy-start.3 = (bf16[64,384]{1,0:T(8,128)(2,1)S(1)}, bf16[64,384]{1,0:T(8,128)(2,1)}, u32[]{:S(2)}) copy-start(bf16[64,384]{1,0:T(8,128)(2,1)} %constant.78.clone.back_ref) | copy-start | bytes 147460

commit v3 on v2

--- a/solution.py
+++ b/solution.py
@@ -16,7 +16,7 @@
 TAPS = 7
 LANES = ROWS // 2
 SENT = 6 * OWN
-BACK = 2 * OWN
+BACK = 2 * OWN + 2
 HOLD = 7000
 SIDE_LEN = 8
 LEAD = 42
@@ -84,6 +84,16 @@
     return jnp.where(code < 0.0, -size, size)
 
 
+def encode_scaled(value, scale):
+    code = jnp.exp2(jnp.abs(value) * (-2.0 * CODE_LOW / scale) + CODE_LOW)
+    return jnp.where(value < 0.0, -code, code)
+
+
+def decode_scaled(code, scale):
+    size = (jnp.log2(jnp.abs(code)) - CODE_LOW) * (scale * (-0.5 / CODE_LOW))
+    return jnp.where(code < 0.0, -size, size)
+
+
 def pack_kernel(hold_ref, key_ref, value_ref, long_ref, out_ref, stage_ref):
     parts = (
         key_ref[...].astype(f32).T,
@@ -101,7 +111,7 @@
 
 
 def filter_kernel(
-    got_ref, taps_ref, gain_ref, outer_ref, back_ref, twist_ref, inner_ref, out_ref, stage_ref
+    got_ref, taps_ref, gain_ref, outer_ref, back_ref, twist_ref, inner_ref, out_ref, stage_ref, send_ref
 ):
     stage_ref[...] = got_ref[...].astype(f32)
     twist_real = twist_ref[0]
@@ -186,18 +196,37 @@
         jnp.concatenate([jnp.concatenate(real, axis=1), jnp.concatenate(imag, axis=1)], axis=0)
     )
     mixed = dot(back_ref[...], jnp.concatenate([high, high, low], axis=0))
-    for i in range(2 * OWN):
-        out_ref[pl.ds(i, BLOCKS, stride=BACK), :] = (
-            mixed[:, i * LANES : (i + 1) * LANES] + gain_ref[i // 2] * turned(gated[i], -TURN)
-        )
-
-
-def finish_kernel(got_ref, query_ref, out_ref):
+    lane = lax.broadcasted_iota(jnp.int32, (BLOCKS, LANES), 1)
+    scales = jnp.ones((BLOCKS, LANES), f32)
+    for own in range(OWN):
+        total = []
+        for i in (2 * own, 2 * own + 1):
+            here = turned(gated[i], -TURN)
+            total.append(mixed[:, i * LANES : (i + 1) * LANES] + gain_ref[own] * here)
+        peak = jnp.maximum(jnp.abs(total[0]), jnp.abs(total[1]))
+        scale = jnp.max(peak, axis=1, keepdims=True) * (1.0 + 2.0**-7) + 1e-30
+        scale = scale.astype(bf16).astype(f32)
+        scales = jnp.where(lane // (LANES // OWN) == own, scale, scales)
+        for part in range(2):
+            code = encode_scaled(total[part], scale)
+            send_ref[pl.ds(2 * own + part, BLOCKS, stride=BACK), :] = code
+    send_ref[pl.ds(2 * OWN, BLOCKS, stride=BACK), :] = scales
+    send_ref[pl.ds(2 * OWN + 1, BLOCKS, stride=BACK), :] = scales
+    out_ref[...] = send_ref[...].astype(bf16)
+
+
+def finish_kernel(got_ref, query_ref, out_ref, stage_ref):
+    stage_ref[...] = got_ref[...].astype(f32)
+    scales = stage_ref[pl.ds(2 * OWN, BLOCKS, stride=BACK), :]
     rows = []
     for own in range(OWN):
-        early = got_ref[pl.ds(2 * own, BLOCKS, stride=BACK), :]
-        late = got_ref[pl.ds(2 * own + 1, BLOCKS, stride=BACK), :]
-        rows.append(jnp.concatenate([turned(early, TURN), turned(late, TURN)], axis=1))
+        lead = own * (LANES // OWN)
+        scale = scales[:, lead : lead + 1]
+        parts = []
+        for i in (2 * own, 2 * own + 1):
+            value = decode_scaled(stage_ref[pl.ds(i, BLOCKS, stride=BACK), :], scale)
+            parts.append(turned(value, TURN))
+        rows.append(jnp.concatenate(parts, axis=1))
     out_ref[...] = (query_ref[...] * jnp.concatenate(rows, axis=0).T).astype(bf16)
 
 
@@ -219,8 +248,10 @@
 
 
 def exchange(blocks, lead):
+    rows = blocks.shape[0] // BLOCKS
+    shape = (BLOCKS, rows, LANES) if rows % 8 == 0 else (BLOCKS, rows // 2, 2, LANES)
     moved = lax.all_to_all(
-        blocks.reshape(BLOCKS, -1, LANES),
+        blocks.reshape(shape),
         "seq",
         split_axis=0,
         concat_axis=0,
@@ -255,10 +286,13 @@
     own_gain = lax.dynamic_index_in_dim(skip_gain.reshape(OWN, BLOCKS), place, 1, keepdims=False)
     mixed = pl.pallas_call(
         filter_kernel,
-        out_shape=pltpu.VMEM((BLOCKS * BACK, LANES), f32),
+        out_shape=pltpu.VMEM((BLOCKS * BACK, LANES), bf16),
         in_specs=in_vmem(1) + [pl.BlockSpec(memory_space=pltpu.SMEM)] * 2 + in_vmem(4),
         out_specs=in_vmem(1)[0],
-        scratch_shapes=[pltpu.VMEM((BLOCKS * SENT, LANES), f32)],
+        scratch_shapes=[
+            pltpu.VMEM((BLOCKS * SENT, LANES), f32),
+            pltpu.VMEM((BLOCKS * BACK, LANES), f32),
+        ],
         name="filter",
     )(near(got), own_taps, own_gain, near(outer), near(outer_back), near(twist), near(inner))
     back = exchange(mixed, LEAD_BACK)
@@ -267,6 +301,7 @@
         out_shape=jax.ShapeDtypeStruct(query_branch.shape, bf16),
         in_specs=in_vmem(2),
         out_specs=in_vmem(1)[0],
+        scratch_shapes=[pltpu.VMEM((BLOCKS * BACK, LANES), f32)],
         name="finish",
     )(near(back), near(query_mix))
 

time: 70.2 us -> 68.2 us (0.972)
  blocking collectives: 22.6 us -> 20.5 us
    all_to_all x1, blocking collectives: 22.6 us -> 20.5 us  [exchange(): lax.all_to_all(blocks.reshape(shape), 'seq', split_axis=0, concat_axis=0,...]
where the time goes in v3:
time: 68.2 us; the launch traced here: 67.8 us
  starting transfers between devices  23.2 us (34%)
  blocking collectives  20.5 us (30%)
  Pallas kernels  14.2 us (21%)
  waiting for transfers between devices  6.27 us (9%)
  local copies, waits for them, and re-layouts  3.22 us (5%)
    all_to_all x1, starting transfers between devices, exchange(): lax.all_to_all(blocks.reshape(shape), 'seq', split_axis=0, concat_axis=0,...  21.3 us
    all_to_all x1, blocking collectives, exchange(): lax.all_to_all(blocks.reshape(shape), 'seq', split_axis=0, concat_axis=0,...  20.5 us
    pallas_call x1, Pallas kernels, shards(): pl.pallas_call(pack_kernel, out_shape=pltpu.VMEM((BLOCKS * SENT, LANES),...  9.11 us
    all_to_all x1, waiting for transfers between devices, exchange(): lax.all_to_all(blocks.reshape(shape), 'seq', split_axis=0, concat_axis=0,...  6.26 us
    pallas_call x1, Pallas kernels, shards(): pl.pallas_call(filter_kernel, out_shape=pltpu.VMEM((BLOCKS * BACK, LANES)...  4.24 us
    ppermute x1, starting transfers between devices, shards(): lax.ppermute(query_branch[-(TAPS - 1):], 'seq', [(i, i + 1) for i in rang...  1.92 us
  transfers between devices with their start and end apart: 2, of which 1 were waited for; matrix products, arithmetic and copies ran while one was open for 3% of the time, Pallas kernels for 0%

profile of v3, /device:TPU:6, one launch (start us, length us, event | category | flops | bytes accessed | tf_op | source)
XLA Modules:
  0.0 67.8 jit_solution(14226193034647022423)
XLA Ops:
  0.0 9.1 %pack.1 = bf16[1536,128]{1,0:T(8,128)(2,1)} custom-call(s32[1]{0:T(128)} %bitcast.hold_ref, bf16[256,256]{1,0:T(8,128)(2,1)} %key_ref.1, bf16[256,256]{1,0:T(8,128)(2,1)} %value_ref.1, f32[256,256]{1,0:T(8,128)} %long_ref.1), custom_call_target="tpu_custom_call" | custom-call | tf_op jit(solution)/shard_map/pack/pallas_call | solution.py:271
  9.1 0.0 copy-start.4
  9.1 21.3 %all-to-all-start = ((bf16[64,24,128]{2,1,0:T(8,128)(2,1)}), bf16[64,24,128]{2,1,0:T(8,128)(2,1)S(1)}, u32[]{:S(2)}, u32[]{:S(2)}) async-start(bf16[64,24,128]{2,1,0:T(8,128)(2,1)} %bitcast.1), calls=%async_computation | async-start | bytes 786432 | tf_op jit(solution)/shard_map/all_to_all | solution.py:253
  30.4 0.0 copy-done.4
  30.4 1.9 %collective-permute-start = (bf16[6,256]{1,0:T(8,128)(2,1)S(1)}, bf16[6,256]{1,0:T(8,128)(2,1)S(1)}, u32[]{:S(2)}, u32[]{:S(2)}) collective-permute-start(bf16[6,256]{1,0:T(8,128)(2,1)S(1)} %slice.64), channel_id=1, source_target_pairs={{0,8},{8,16},{16,24},{24,32},{32,40},{40,48},{48,56},{56,64},{64,7... | collective-permute-start | bytes 9224 | tf_op jit(solution)/shard_map/ppermute | solution.py:266
  32.4 0.0 slice-start
  32.4 0.7 %slice-done = f32[2,7,256]{2,1,0:T(8,128)S(1)} async-done(((f32[3,7,256]{2,1,0:T(8,128)}), f32[2,7,256]{2,1,0:T(8,128)S(1)}, s32[]{:S(2)}) %slice-start) | async-done | bytes 14360 | tf_op jit(solution)/shard_map/slice | solution.py:284
  33.1 0.0 copy-start.5
  33.1 0.1 reshape.34
  33.2 0.7 copy-done.5
  33.9 0.1 constant_dynamic-slice_fusion
  34.0 0.1 copy.17
  34.1 0.0 copy-start.6
  34.1 0.7 %copy.16.taps_ref = f32[2,7,4]{2,1,0:T(8,128)} copy(f32[2,7,4]{1,2,0:T(4,128)S(1)} %bitcast.16) | data formatting | bytes 448 | tf_op jit(solution)/shard_map/jit(dynamic_index_in_dim)/squeeze | solution.py:283
  34.8 0.0 copy-done.6
  34.8 0.1 reshape.35
  34.9 0.7 %dynamic-slice_reduce_fusion.gain_ref = f32[4]{0:T(128)} fusion(f32[4,64]{1,0:T(4,128)S(1)} %reshape.35, s32[]{:T(128)S(6)} %select_n.29), kind=kLoop, calls=%fused_computation.14 | loop fusion | bytes 36 | tf_op jit(solution)/shard_map/jit(dynamic_index_in_dim)/dynamic_slice | solution.py:286
  35.6 0.0 collective-permute-done
  35.6 0.0 copy-start
  35.7 0.0 copy-start.1
  35.7 0.0 copy-start.2
  35.7 0.0 copy-start.3
  35.7 0.2 fusion.query_ref
  35.9 6.3 %all-to-all-done = bf16[64,24,128]{2,1,0:T(8,128)(2,1)S(1)} async-done(((bf16[64,24,128]{2,1,0:T(8,128)(2,1)}), bf16[64,24,128]{2,1,0:T(8,128)(2,1)S(1)}, u32[]{:S(2)}, u32[]{:S(2)}) %all-to-all-start) | async-done | bytes 393248 | tf_op jit(solution)/shard_map/all_to_all | solution.py:253
  42.2 0.0 copy-done
  42.2 0.0 copy-done.1
  42.2 0.0 copy-done.2
  42.2 0.0 copy-done.3
  42.2 4.2 %filter.1 = bf16[640,128]{1,0:T(8,128)(2,1)S(1)} custom-call(bf16[1536,128]{1,0:T(8,128)(2,1)S(1)} %bitcast.13, f32[2,7,4]{2,1,0:T(8,128)} %copy.16.taps_ref, f32[4]{0:T(128)} %dynamic-slice_reduce_fusion.gain_ref, bf16[128,192]{1,0:T(8,128)(2,1)S(1)} %copy-done.2, bf16[64,384]{1,0:T(8,128)(2,1)S(1)} %copy-done.3, f32[2,64,256]{2,1,0:T(8,128)S(1)} %copy-done.1, ...), custom_call_target="tpu_custom_call" | custom-call | tf_op jit(solution)/shard_map/filter/pallas_call | solution.py:287
  46.5 20.5 %all_to_all.10 = bf16[64,5,2,128]{3,2,1,0:T(2,128)(2,1)S(1)} all-to-all(bf16[64,5,2,128]{3,2,1,0:T(2,128)(2,1)S(1)} %bitcast.14), channel_id=1, replica_groups={{272,336,400,464,16,80,144,208,280,344,408,472,24,88,152,216,288,352,41..., dimensions={0} | all-to-all | bytes 327680 | tf_op jit(solution)/shard_map/all_to_all | solution.py:253
  66.9 0.9 %finish.1 = bf16[256,256]{1,0:T(8,128)(2,1)} custom-call(bf16[640,128]{1,0:T(8,128)(2,1)S(1)} %bitcast.15, f32[256,256]{1,0:T(8,128)S(1)} %fusion.query_ref), custom_call_target="tpu_custom_call" | custom-call | tf_op jit(solution)/shard_map/finish/pallas_call | solution.py:299
  (3 shorter events, 0.0 us)
Async XLA Ops:
  9.1 21.3 %copy-start.4 = (bf16[256,256]{1,0:T(8,128)(2,1)S(1)}, bf16[256,256]{1,0:T(8,128)(2,1)}, u32[]{:S(2)}) copy-start(bf16[256,256]{1,0:T(8,128)(2,1)} %param.10) | copy-start | bytes 393220
  9.1 33.1 %all-to-all-start = ((bf16[64,24,128]{2,1,0:T(8,128)(2,1)}), bf16[64,24,128]{2,1,0:T(8,128)(2,1)S(1)}, u32[]{:S(2)}, u32[]{:S(2)}) async-start(bf16[64,24,128]{2,1,0:T(8,128)(2,1)} %bitcast.1), calls=%async_computation | async-start | bytes 786432 | tf_op jit(solution)/shard_map/all_to_all | solution.py:253
  30.4 5.2 %collective-permute-start = (bf16[6,256]{1,0:T(8,128)(2,1)S(1)}, bf16[6,256]{1,0:T(8,128)(2,1)S(1)}, u32[]{:S(2)}, u32[]{:S(2)}) collective-permute-start(bf16[6,256]{1,0:T(8,128)(2,1)S(1)} %slice.64), channel_id=1, source_target_pairs={{0,8},{8,16},{16,24},{24,32},{32,40},{40,48},{48,56},{56,64},{64,7... | collective-permute-start | bytes 9224 | tf_op jit(solution)/shard_map/ppermute | solution.py:266
  32.4 0.7 %slice-start = ((f32[3,7,256]{2,1,0:T(8,128)}), f32[2,7,256]{2,1,0:T(8,128)S(1)}, s32[]{:S(2)}) async-start(f32[3,7,256]{2,1,0:T(8,128)} %param.13), calls=%async_computation.2 | async-start | bytes 32768 | tf_op jit(solution)/shard_map/slice | solution.py:284
  33.1 0.7 %copy-start.5 = (f32[3,7,256]{2,1,0:T(8,128)S(1)}, f32[3,7,256]{2,1,0:T(8,128)}, u32[]{:S(2)}) copy-start(f32[3,7,256]{2,1,0:T(8,128)} %param.13) | copy-start | bytes 64516
  34.1 0.7 %copy-start.6 = (f32[256]{0:T(256)S(1)}, f32[256]{0:T(256)}, u32[]{:S(2)}) copy-start(f32[256]{0:T(256)} %param.15) | copy-start | bytes 3076
  35.6 6.5 %copy-start = (bf16[2,256,512]{2,1,0:T(8,128)(2,1)S(1)}, bf16[2,256,512]{2,1,0:T(8,128)(2,1)}, u32[]{:S(2)}) copy-start(bf16[2,256,512]{2,1,0:T(8,128)(2,1)} %constant.80.clone.inner_ref) | copy-start | bytes 1572868
  35.7 6.5 %copy-start.1 = (f32[2,64,256]{2,1,0:T(8,128)S(1)}, f32[2,64,256]{2,1,0:T(8,128)}, u32[]{:S(2)}) copy-start(f32[2,64,256]{2,1,0:T(8,128)} %constant.79.clone.twist_ref) | copy-start | bytes 393220
  35.7 6.5 %copy-start.2 = (bf16[128,192]{1,0:T(8,128)(2,1)S(1)}, bf16[128,192]{1,0:T(8,128)(2,1)}, u32[]{:S(2)}) copy-start(bf16[128,192]{1,0:T(8,128)(2,1)} %constant.77.clone.outer_ref) | copy-start | bytes 147460
  35.7 6.5 %copy-start.3 = (bf16[64,384]{1,0:T(8,128)(2,1)S(1)}, bf16[64,384]{1,0:T(8,128)(2,1)}, u32[]{:S(2)}) copy-start(bf16[64,384]{1,0:T(8,128)(2,1)} %constant.78.clone.back_ref) | copy-start | bytes 147460

commit v4 on v3

--- a/solution.py
+++ b/solution.py
@@ -118,14 +118,18 @@
     twist_imag = twist_ref[1]
     inner_high = inner_ref[0]
     inner_low = inner_ref[1]
+    inner_all = jnp.concatenate([inner_high, inner_low, inner_high], axis=0)
     half = OWN * BLOCKS
 
     def staged(row):
         return stage_ref[pl.ds(row, BLOCKS, stride=SENT), :]
 
     def inner_product(value):
-        high, low = split(value)
-        return dot(high, inner_high) + dot(high, inner_low) + dot(low, inner_high)
+        parts = []
+        for i in range(2):
+            high, low = split(value[i * half : (i + 1) * half])
+            parts.append(dot(jnp.concatenate([high, high, low], axis=1), inner_all))
+        return jnp.concatenate(parts, axis=0)
 
     def spectrum(signal):
         high, low = split(signal)

time: 68.2 us -> 67.8 us (level)
  no operation moved by 1% of the time
where the time goes in v4:
time: 67.8 us; the launch traced here: 67.3 us
  starting transfers between devices  23.2 us (34%)
  blocking collectives  20.5 us (30%)
  Pallas kernels  13.8 us (20%)
  waiting for transfers between devices  6.27 us (9%)
  local copies, waits for them, and re-layouts  3.22 us (5%)
    all_to_all x1, starting transfers between devices, exchange(): lax.all_to_all(blocks.reshape(shape), 'seq', split_axis=0, concat_axis=0,...  21.3 us
    all_to_all x1, blocking collectives, exchange(): lax.all_to_all(blocks.reshape(shape), 'seq', split_axis=0, concat_axis=0,...  20.5 us
    pallas_call x1, Pallas kernels, shards(): pl.pallas_call(pack_kernel, out_shape=pltpu.VMEM((BLOCKS * SENT, LANES),...  9.11 us
    all_to_all x1, waiting for transfers between devices, exchange(): lax.all_to_all(blocks.reshape(shape), 'seq', split_axis=0, concat_axis=0,...  6.26 us
    pallas_call x1, Pallas kernels, shards(): pl.pallas_call(filter_kernel, out_shape=pltpu.VMEM((BLOCKS * BACK, LANES)...  3.77 us
    ppermute x1, starting transfers between devices, shards(): lax.ppermute(query_branch[-(TAPS - 1):], 'seq', [(i, i + 1) for i in rang...  1.92 us
  transfers between devices with their start and end apart: 2, of which 1 were waited for; matrix products, arithmetic and copies ran while one was open for 3% of the time, Pallas kernels for 0%

profile of v4, /device:TPU:6, one launch (start us, length us, event | category | flops | bytes accessed | tf_op | source)
XLA Modules:
  0.0 67.3 jit_solution(14617127417084999363)
XLA Ops:
  0.0 9.1 %pack.1 = bf16[1536,128]{1,0:T(8,128)(2,1)} custom-call(s32[1]{0:T(128)} %bitcast.hold_ref, bf16[256,256]{1,0:T(8,128)(2,1)} %key_ref.1, bf16[256,256]{1,0:T(8,128)(2,1)} %value_ref.1, f32[256,256]{1,0:T(8,128)} %long_ref.1), custom_call_target="tpu_custom_call" | custom-call | tf_op jit(solution)/shard_map/pack/pallas_call | solution.py:275
  9.1 0.0 copy-start.4
  9.1 21.3 %all-to-all-start = ((bf16[64,24,128]{2,1,0:T(8,128)(2,1)}), bf16[64,24,128]{2,1,0:T(8,128)(2,1)S(1)}, u32[]{:S(2)}, u32[]{:S(2)}) async-start(bf16[64,24,128]{2,1,0:T(8,128)(2,1)} %bitcast.1), calls=%async_computation | async-start | bytes 786432 | tf_op jit(solution)/shard_map/all_to_all | solution.py:257
  30.4 0.0 copy-done.4
  30.4 1.9 %collective-permute-start = (bf16[6,256]{1,0:T(8,128)(2,1)S(1)}, bf16[6,256]{1,0:T(8,128)(2,1)S(1)}, u32[]{:S(2)}, u32[]{:S(2)}) collective-permute-start(bf16[6,256]{1,0:T(8,128)(2,1)S(1)} %slice.64), channel_id=1, source_target_pairs={{0,8},{8,16},{16,24},{24,32},{32,40},{40,48},{48,56},{56,64},{64,7... | collective-permute-start | bytes 9224 | tf_op jit(solution)/shard_map/ppermute | solution.py:270
  32.4 0.0 slice-start
  32.4 0.7 %slice-done = f32[2,7,256]{2,1,0:T(8,128)S(1)} async-done(((f32[3,7,256]{2,1,0:T(8,128)}), f32[2,7,256]{2,1,0:T(8,128)S(1)}, s32[]{:S(2)}) %slice-start) | async-done | bytes 14360 | tf_op jit(solution)/shard_map/slice | solution.py:288
  33.1 0.0 copy-start.5
  33.1 0.1 reshape.34
  33.2 0.7 copy-done.5
  33.9 0.1 constant_dynamic-slice_fusion
  34.0 0.1 copy.17
  34.1 0.0 copy-start.6
  34.1 0.7 %copy.16.taps_ref = f32[2,7,4]{2,1,0:T(8,128)} copy(f32[2,7,4]{1,2,0:T(4,128)S(1)} %bitcast.16) | data formatting | bytes 448 | tf_op jit(solution)/shard_map/jit(dynamic_index_in_dim)/squeeze | solution.py:287
  34.8 0.0 copy-done.6
  34.8 0.1 reshape.35
  34.9 0.7 %dynamic-slice_reduce_fusion.gain_ref = f32[4]{0:T(128)} fusion(f32[4,64]{1,0:T(4,128)S(1)} %reshape.35, s32[]{:T(128)S(6)} %select_n.29), kind=kLoop, calls=%fused_computation.14 | loop fusion | bytes 36 | tf_op jit(solution)/shard_map/jit(dynamic_index_in_dim)/dynamic_slice | solution.py:290
  35.6 0.0 collective-permute-done
  35.6 0.0 copy-start
  35.7 0.0 copy-start.1
  35.7 0.0 copy-start.2
  35.7 0.0 copy-start.3
  35.7 0.2 fusion.query_ref
  35.9 6.3 %all-to-all-done = bf16[64,24,128]{2,1,0:T(8,128)(2,1)S(1)} async-done(((bf16[64,24,128]{2,1,0:T(8,128)(2,1)}), bf16[64,24,128]{2,1,0:T(8,128)(2,1)S(1)}, u32[]{:S(2)}, u32[]{:S(2)}) %all-to-all-start) | async-done | bytes 393248 | tf_op jit(solution)/shard_map/all_to_all | solution.py:257
  42.2 0.0 copy-done
  42.2 0.0 copy-done.1
  42.2 0.0 copy-done.2
  42.2 0.0 copy-done.3
  42.2 3.8 %filter.1 = bf16[640,128]{1,0:T(8,128)(2,1)S(1)} custom-call(bf16[1536,128]{1,0:T(8,128)(2,1)S(1)} %bitcast.13, f32[2,7,4]{2,1,0:T(8,128)} %copy.16.taps_ref, f32[4]{0:T(128)} %dynamic-slice_reduce_fusion.gain_ref, bf16[128,192]{1,0:T(8,128)(2,1)S(1)} %copy-done.2, bf16[64,384]{1,0:T(8,128)(2,1)S(1)} %copy-done.3, f32[2,64,256]{2,1,0:T(8,128)S(1)} %copy-done.1, ...), custom_call_target="tpu_custom_call" | custom-call | tf_op jit(solution)/shard_map/filter/pallas_call | solution.py:291
  46.0 20.5 %all_to_all.10 = bf16[64,5,2,128]{3,2,1,0:T(2,128)(2,1)S(1)} all-to-all(bf16[64,5,2,128]{3,2,1,0:T(2,128)(2,1)S(1)} %bitcast.14), channel_id=1, replica_groups={{272,336,400,464,16,80,144,208,280,344,408,472,24,88,152,216,288,352,41..., dimensions={0} | all-to-all | bytes 327680 | tf_op jit(solution)/shard_map/all_to_all | solution.py:257
  66.4 0.9 %finish.1 = bf16[256,256]{1,0:T(8,128)(2,1)} custom-call(bf16[640,128]{1,0:T(8,128)(2,1)S(1)} %bitcast.15, f32[256,256]{1,0:T(8,128)S(1)} %fusion.query_ref), custom_call_target="tpu_custom_call" | custom-call | tf_op jit(solution)/shard_map/finish/pallas_call | solution.py:303
  (3 shorter events, 0.0 us)
Async XLA Ops:
  9.1 21.3 %copy-start.4 = (bf16[256,256]{1,0:T(8,128)(2,1)S(1)}, bf16[256,256]{1,0:T(8,128)(2,1)}, u32[]{:S(2)}) copy-start(bf16[256,256]{1,0:T(8,128)(2,1)} %param.10) | copy-start | bytes 393220
  9.1 33.1 %all-to-all-start = ((bf16[64,24,128]{2,1,0:T(8,128)(2,1)}), bf16[64,24,128]{2,1,0:T(8,128)(2,1)S(1)}, u32[]{:S(2)}, u32[]{:S(2)}) async-start(bf16[64,24,128]{2,1,0:T(8,128)(2,1)} %bitcast.1), calls=%async_computation | async-start | bytes 786432 | tf_op jit(solution)/shard_map/all_to_all | solution.py:257
  30.4 5.2 %collective-permute-start = (bf16[6,256]{1,0:T(8,128)(2,1)S(1)}, bf16[6,256]{1,0:T(8,128)(2,1)S(1)}, u32[]{:S(2)}, u32[]{:S(2)}) collective-permute-start(bf16[6,256]{1,0:T(8,128)(2,1)S(1)} %slice.64), channel_id=1, source_target_pairs={{0,8},{8,16},{16,24},{24,32},{32,40},{40,48},{48,56},{56,64},{64,7... | collective-permute-start | bytes 9224 | tf_op jit(solution)/shard_map/ppermute | solution.py:270
  32.4 0.7 %slice-start = ((f32[3,7,256]{2,1,0:T(8,128)}), f32[2,7,256]{2,1,0:T(8,128)S(1)}, s32[]{:S(2)}) async-start(f32[3,7,256]{2,1,0:T(8,128)} %param.13), calls=%async_computation.2 | async-start | bytes 32768 | tf_op jit(solution)/shard_map/slice | solution.py:288
  33.1 0.7 %copy-start.5 = (f32[3,7,256]{2,1,0:T(8,128)S(1)}, f32[3,7,256]{2,1,0:T(8,128)}, u32[]{:S(2)}) copy-start(f32[3,7,256]{2,1,0:T(8,128)} %param.13) | copy-start | bytes 64516
  34.1 0.7 %copy-start.6 = (f32[256]{0:T(256)S(1)}, f32[256]{0:T(256)}, u32[]{:S(2)}) copy-start(f32[256]{0:T(256)} %param.15) | copy-start | bytes 3076
  35.6 6.5 %copy-start = (bf16[2,256,512]{2,1,0:T(8,128)(2,1)S(1)}, bf16[2,256,512]{2,1,0:T(8,128)(2,1)}, u32[]{:S(2)}) copy-start(bf16[2,256,512]{2,1,0:T(8,128)(2,1)} %constant.80.clone.inner_ref) | copy-start | bytes 1572868
  35.7 6.5 %copy-start.1 = (f32[2,64,256]{2,1,0:T(8,128)S(1)}, f32[2,64,256]{2,1,0:T(8,128)}, u32[]{:S(2)}) copy-start(f32[2,64,256]{2,1,0:T(8,128)} %constant.79.clone.twist_ref) | copy-start | bytes 393220
  35.7 6.5 %copy-start.2 = (bf16[128,192]{1,0:T(8,128)(2,1)S(1)}, bf16[128,192]{1,0:T(8,128)(2,1)}, u32[]{:S(2)}) copy-start(bf16[128,192]{1,0:T(8,128)(2,1)} %constant.77.clone.outer_ref) | copy-start | bytes 147460
  35.7 6.5 %copy-start.3 = (bf16[64,384]{1,0:T(8,128)(2,1)S(1)}, bf16[64,384]{1,0:T(8,128)(2,1)}, u32[]{:S(2)}) copy-start(bf16[64,384]{1,0:T(8,128)(2,1)} %constant.78.clone.back_ref) | copy-start | bytes 147460

commit v5 on v4

--- a/solution.py
+++ b/solution.py
@@ -32,9 +32,9 @@
 START_GROUP = -LEAD % SIDE_LEN
 START_ROW = -LEAD % BLOCKS // SIDE_LEN
 
-FLOOR = 2.0**-10
+FLOOR = 2.0**-9
 CODE_LOW = -125.0
-CODE_RATE = 250.0 / np.log2(1.0 + 1.6 / FLOOR)
+CODE_RATE = 250.0 / np.log2(1.0 + 1.55 / FLOOR)
 
 
 def halves(table):

time: 67.8 us -> 67.8 us (level)
  no operation moved by 1% of the time
where the time goes in v5:
time: 67.8 us; the launch traced here: 67.3 us
  starting transfers between devices  23.2 us (34%)
  blocking collectives  20.5 us (30%)
  Pallas kernels  13.8 us (20%)
  waiting for transfers between devices  6.27 us (9%)
  local copies, waits for them, and re-layouts  3.22 us (5%)
    all_to_all x1, starting transfers between devices, exchange(): lax.all_to_all(blocks.reshape(shape), 'seq', split_axis=0, concat_axis=0,...  21.3 us
    all_to_all x1, blocking collectives, exchange(): lax.all_to_all(blocks.reshape(shape), 'seq', split_axis=0, concat_axis=0,...  20.5 us
    pallas_call x1, Pallas kernels, shards(): pl.pallas_call(pack_kernel, out_shape=pltpu.VMEM((BLOCKS * SENT, LANES),...  9.11 us
    all_to_all x1, waiting for transfers between devices, exchange(): lax.all_to_all(blocks.reshape(shape), 'seq', split_axis=0, concat_axis=0,...  6.26 us
    pallas_call x1, Pallas kernels, shards(): pl.pallas_call(filter_kernel, out_shape=pltpu.VMEM((BLOCKS * BACK, LANES)...  3.77 us
    ppermute x1, starting transfers between devices, shards(): lax.ppermute(query_branch[-(TAPS - 1):], 'seq', [(i, i + 1) for i in rang...  1.92 us
  transfers between devices with their start and end apart: 2, of which 1 were waited for; matrix products, arithmetic and copies ran while one was open for 3% of the time, Pallas kernels for 0%

profile of v5, /device:TPU:6, one launch (start us, length us, event | category | flops | bytes accessed | tf_op | source)
XLA Modules:
  0.0 67.3 jit_solution(8794767799117764357)
XLA Ops:
  0.0 9.1 %pack.1 = bf16[1536,128]{1,0:T(8,128)(2,1)} custom-call(s32[1]{0:T(128)} %bitcast.hold_ref, bf16[256,256]{1,0:T(8,128)(2,1)} %key_ref.1, bf16[256,256]{1,0:T(8,128)(2,1)} %value_ref.1, f32[256,256]{1,0:T(8,128)} %long_ref.1), custom_call_target="tpu_custom_call" | custom-call | tf_op jit(solution)/shard_map/pack/pallas_call | solution.py:275
  9.1 0.0 copy-start.4
  9.1 21.3 %all-to-all-start = ((bf16[64,24,128]{2,1,0:T(8,128)(2,1)}), bf16[64,24,128]{2,1,0:T(8,128)(2,1)S(1)}, u32[]{:S(2)}, u32[]{:S(2)}) async-start(bf16[64,24,128]{2,1,0:T(8,128)(2,1)} %bitcast.1), calls=%async_computation | async-start | bytes 786432 | tf_op jit(solution)/shard_map/all_to_all | solution.py:257
  30.4 0.0 copy-done.4
  30.4 1.9 %collective-permute-start = (bf16[6,256]{1,0:T(8,128)(2,1)S(1)}, bf16[6,256]{1,0:T(8,128)(2,1)S(1)}, u32[]{:S(2)}, u32[]{:S(2)}) collective-permute-start(bf16[6,256]{1,0:T(8,128)(2,1)S(1)} %slice.64), channel_id=1, source_target_pairs={{0,8},{8,16},{16,24},{24,32},{32,40},{40,48},{48,56},{56,64},{64,7... | collective-permute-start | bytes 9224 | tf_op jit(solution)/shard_map/ppermute | solution.py:270
  32.4 0.0 slice-start
  32.4 0.7 %slice-done = f32[2,7,256]{2,1,0:T(8,128)S(1)} async-done(((f32[3,7,256]{2,1,0:T(8,128)}), f32[2,7,256]{2,1,0:T(8,128)S(1)}, s32[]{:S(2)}) %slice-start) | async-done | bytes 14360 | tf_op jit(solution)/shard_map/slice | solution.py:288
  33.1 0.0 copy-start.5
  33.1 0.1 reshape.34
  33.2 0.7 copy-done.5
  33.9 0.1 constant_dynamic-slice_fusion
  34.0 0.1 copy.17
  34.1 0.0 copy-start.6
  34.1 0.7 %copy.16.taps_ref = f32[2,7,4]{2,1,0:T(8,128)} copy(f32[2,7,4]{1,2,0:T(4,128)S(1)} %bitcast.16) | data formatting | bytes 448 | tf_op jit(solution)/shard_map/jit(dynamic_index_in_dim)/squeeze | solution.py:287
  34.8 0.0 copy-done.6
  34.8 0.1 reshape.35
  34.9 0.7 %dynamic-slice_reduce_fusion.gain_ref = f32[4]{0:T(128)} fusion(f32[4,64]{1,0:T(4,128)S(1)} %reshape.35, s32[]{:T(128)S(6)} %select_n.29), kind=kLoop, calls=%fused_computation.14 | loop fusion | bytes 36 | tf_op jit(solution)/shard_map/jit(dynamic_index_in_dim)/dynamic_slice | solution.py:290
  35.6 0.0 collective-permute-done
  35.6 0.0 copy-start
  35.7 0.0 copy-start.1
  35.7 0.0 copy-start.2
  35.7 0.0 copy-start.3
  35.7 0.2 fusion.query_ref
  35.9 6.3 %all-to-all-done = bf16[64,24,128]{2,1,0:T(8,128)(2,1)S(1)} async-done(((bf16[64,24,128]{2,1,0:T(8,128)(2,1)}), bf16[64,24,128]{2,1,0:T(8,128)(2,1)S(1)}, u32[]{:S(2)}, u32[]{:S(2)}) %all-to-all-start) | async-done | bytes 393248 | tf_op jit(solution)/shard_map/all_to_all | solution.py:257
  42.2 0.0 copy-done
  42.2 0.0 copy-done.1
  42.2 0.0 copy-done.2
  42.2 0.0 copy-done.3
  42.2 3.8 %filter.1 = bf16[640,128]{1,0:T(8,128)(2,1)S(1)} custom-call(bf16[1536,128]{1,0:T(8,128)(2,1)S(1)} %bitcast.13, f32[2,7,4]{2,1,0:T(8,128)} %copy.16.taps_ref, f32[4]{0:T(128)} %dynamic-slice_reduce_fusion.gain_ref, bf16[128,192]{1,0:T(8,128)(2,1)S(1)} %copy-done.2, bf16[64,384]{1,0:T(8,128)(2,1)S(1)} %copy-done.3, f32[2,64,256]{2,1,0:T(8,128)S(1)} %copy-done.1, ...), custom_call_target="tpu_custom_call" | custom-call | tf_op jit(solution)/shard_map/filter/pallas_call | solution.py:291
  46.0 20.5 %all_to_all.10 = bf16[64,5,2,128]{3,2,1,0:T(2,128)(2,1)S(1)} all-to-all(bf16[64,5,2,128]{3,2,1,0:T(2,128)(2,1)S(1)} %bitcast.14), channel_id=1, replica_groups={{272,336,400,464,16,80,144,208,280,344,408,472,24,88,152,216,288,352,41..., dimensions={0} | all-to-all | bytes 327680 | tf_op jit(solution)/shard_map/all_to_all | solution.py:257
  66.4 0.9 %finish.1 = bf16[256,256]{1,0:T(8,128)(2,1)} custom-call(bf16[640,128]{1,0:T(8,128)(2,1)S(1)} %bitcast.15, f32[256,256]{1,0:T(8,128)S(1)} %fusion.query_ref), custom_call_target="tpu_custom_call" | custom-call | tf_op jit(solution)/shard_map/finish/pallas_call | solution.py:303
  (3 shorter events, 0.0 us)
Async XLA Ops:
  9.1 21.3 %copy-start.4 = (bf16[256,256]{1,0:T(8,128)(2,1)S(1)}, bf16[256,256]{1,0:T(8,128)(2,1)}, u32[]{:S(2)}) copy-start(bf16[256,256]{1,0:T(8,128)(2,1)} %param.10) | copy-start | bytes 393220
  9.1 33.1 %all-to-all-start = ((bf16[64,24,128]{2,1,0:T(8,128)(2,1)}), bf16[64,24,128]{2,1,0:T(8,128)(2,1)S(1)}, u32[]{:S(2)}, u32[]{:S(2)}) async-start(bf16[64,24,128]{2,1,0:T(8,128)(2,1)} %bitcast.1), calls=%async_computation | async-start | bytes 786432 | tf_op jit(solution)/shard_map/all_to_all | solution.py:257
  30.4 5.2 %collective-permute-start = (bf16[6,256]{1,0:T(8,128)(2,1)S(1)}, bf16[6,256]{1,0:T(8,128)(2,1)S(1)}, u32[]{:S(2)}, u32[]{:S(2)}) collective-permute-start(bf16[6,256]{1,0:T(8,128)(2,1)S(1)} %slice.64), channel_id=1, source_target_pairs={{0,8},{8,16},{16,24},{24,32},{32,40},{40,48},{48,56},{56,64},{64,7... | collective-permute-start | bytes 9224 | tf_op jit(solution)/shard_map/ppermute | solution.py:270
  32.4 0.7 %slice-start = ((f32[3,7,256]{2,1,0:T(8,128)}), f32[2,7,256]{2,1,0:T(8,128)S(1)}, s32[]{:S(2)}) async-start(f32[3,7,256]{2,1,0:T(8,128)} %param.13), calls=%async_computation.2 | async-start | bytes 32768 | tf_op jit(solution)/shard_map/slice | solution.py:288
  33.1 0.7 %copy-start.5 = (f32[3,7,256]{2,1,0:T(8,128)S(1)}, f32[3,7,256]{2,1,0:T(8,128)}, u32[]{:S(2)}) copy-start(f32[3,7,256]{2,1,0:T(8,128)} %param.13) | copy-start | bytes 64516
  34.1 0.7 %copy-start.6 = (f32[256]{0:T(256)S(1)}, f32[256]{0:T(256)}, u32[]{:S(2)}) copy-start(f32[256]{0:T(256)} %param.15) | copy-start | bytes 3076
  35.6 6.5 %copy-start = (bf16[2,256,512]{2,1,0:T(8,128)(2,1)S(1)}, bf16[2,256,512]{2,1,0:T(8,128)(2,1)}, u32[]{:S(2)}) copy-start(bf16[2,256,512]{2,1,0:T(8,128)(2,1)} %constant.80.clone.inner_ref) | copy-start | bytes 1572868
  35.7 6.5 %copy-start.1 = (f32[2,64,256]{2,1,0:T(8,128)S(1)}, f32[2,64,256]{2,1,0:T(8,128)}, u32[]{:S(2)}) copy-start(f32[2,64,256]{2,1,0:T(8,128)} %constant.79.clone.twist_ref) | copy-start | bytes 393220
  35.7 6.5 %copy-start.2 = (bf16[128,192]{1,0:T(8,128)(2,1)S(1)}, bf16[128,192]{1,0:T(8,128)(2,1)}, u32[]{:S(2)}) copy-start(bf16[128,192]{1,0:T(8,128)(2,1)} %constant.77.clone.outer_ref) | copy-start | bytes 147460
  35.7 6.5 %copy-start.3 = (bf16[64,384]{1,0:T(8,128)(2,1)S(1)}, bf16[64,384]{1,0:T(8,128)(2,1)}, u32[]{:S(2)}) copy-start(bf16[64,384]{1,0:T(8,128)(2,1)} %constant.78.clone.back_ref) | copy-start | bytes 147460

commit v6 on v5

--- a/solution.py
+++ b/solution.py
@@ -17,7 +17,7 @@
 LANES = ROWS // 2
 SENT = 6 * OWN
 BACK = 2 * OWN + 2
-HOLD = 7000
+HOLD = 6000
 SIDE_LEN = 8
 LEAD = 42
 LEAD_BACK = 34

time: 67.8 us -> 67.7 us (level)
  waiting for transfers between devices: 6.27 us -> 7.38 us
  Pallas kernels: 13.8 us -> 12.8 us
    all_to_all x1, waiting for transfers between devices: 6.26 us -> 7.38 us  [exchange(): lax.all_to_all(blocks.reshape(shape), 'seq', split_axis=0, concat_axis=0,...]
    pallas_call x1, Pallas kernels: 9.11 us -> 8.11 us  [shards(): pl.pallas_call(pack_kernel, out_shape=pltpu.VMEM((BLOCKS * SENT, LANES),...]
where the time goes in v6:
time: 67.7 us; the launch traced here: 67.3 us
  starting transfers between devices  23.2 us (34%)
  blocking collectives  20.3 us (30%)
  Pallas kernels  12.8 us (19%)
  waiting for transfers between devices  7.38 us (11%)
  local copies, waits for them, and re-layouts  3.22 us (5%)
    all_to_all x1, starting transfers between devices, exchange(): lax.all_to_all(blocks.reshape(shape), 'seq', split_axis=0, concat_axis=0,...  21.3 us
    all_to_all x1, blocking collectives, exchange(): lax.all_to_all(blocks.reshape(shape), 'seq', split_axis=0, concat_axis=0,...  20.3 us
    pallas_call x1, Pallas kernels, shards(): pl.pallas_call(pack_kernel, out_shape=pltpu.VMEM((BLOCKS * SENT, LANES),...  8.11 us
    all_to_all x1, waiting for transfers between devices, exchange(): lax.all_to_all(blocks.reshape(shape), 'seq', split_axis=0, concat_axis=0,...  7.38 us
    pallas_call x1, Pallas kernels, shards(): pl.pallas_call(filter_kernel, out_shape=pltpu.VMEM((BLOCKS * BACK, LANES)...  3.77 us
    ppermute x1, starting transfers between devices, shards(): lax.ppermute(query_branch[-(TAPS - 1):], 'seq', [(i, i + 1) for i in rang...  1.92 us
  transfers between devices with their start and end apart: 2, of which 1 were waited for; matrix products, arithmetic and copies ran while one was open for 3% of the time, Pallas kernels for 0%

profile of v6, /device:TPU:6, one launch (start us, length us, event | category | flops | bytes accessed | tf_op | source)
XLA Modules:
  0.0 67.3 jit_solution(4038436495114835939)
XLA Ops:
  0.0 8.1 %pack.1 = bf16[1536,128]{1,0:T(8,128)(2,1)} custom-call(s32[1]{0:T(128)} %bitcast.hold_ref, bf16[256,256]{1,0:T(8,128)(2,1)} %key_ref.1, bf16[256,256]{1,0:T(8,128)(2,1)} %value_ref.1, f32[256,256]{1,0:T(8,128)} %long_ref.1), custom_call_target="tpu_custom_call" | custom-call | tf_op jit(solution)/shard_map/pack/pallas_call | solution.py:275
  8.1 0.0 copy-start.4
  8.1 21.3 %all-to-all-start = ((bf16[64,24,128]{2,1,0:T(8,128)(2,1)}), bf16[64,24,128]{2,1,0:T(8,128)(2,1)S(1)}, u32[]{:S(2)}, u32[]{:S(2)}) async-start(bf16[64,24,128]{2,1,0:T(8,128)(2,1)} %bitcast.1), calls=%async_computation | async-start | bytes 786432 | tf_op jit(solution)/shard_map/all_to_all | solution.py:257
  29.4 0.0 copy-done.4
  29.4 1.9 %collective-permute-start = (bf16[6,256]{1,0:T(8,128)(2,1)S(1)}, bf16[6,256]{1,0:T(8,128)(2,1)S(1)}, u32[]{:S(2)}, u32[]{:S(2)}) collective-permute-start(bf16[6,256]{1,0:T(8,128)(2,1)S(1)} %slice.64), channel_id=1, source_target_pairs={{0,8},{8,16},{16,24},{24,32},{32,40},{40,48},{48,56},{56,64},{64,7... | collective-permute-start | bytes 9224 | tf_op jit(solution)/shard_map/ppermute | solution.py:270
  31.4 0.0 slice-start
  31.4 0.7 %slice-done = f32[2,7,256]{2,1,0:T(8,128)S(1)} async-done(((f32[3,7,256]{2,1,0:T(8,128)}), f32[2,7,256]{2,1,0:T(8,128)S(1)}, s32[]{:S(2)}) %slice-start) | async-done | bytes 14360 | tf_op jit(solution)/shard_map/slice | solution.py:288
  32.1 0.0 copy-start.5
  32.1 0.1 reshape.34
  32.2 0.7 copy-done.5
  32.9 0.1 constant_dynamic-slice_fusion
  33.0 0.1 copy.17
  33.1 0.0 copy-start.6
  33.1 0.7 %copy.16.taps_ref = f32[2,7,4]{2,1,0:T(8,128)} copy(f32[2,7,4]{1,2,0:T(4,128)S(1)} %bitcast.16) | data formatting | bytes 448 | tf_op jit(solution)/shard_map/jit(dynamic_index_in_dim)/squeeze | solution.py:287
  33.8 0.0 copy-done.6
  33.8 0.1 reshape.35
  33.9 0.7 %dynamic-slice_reduce_fusion.gain_ref = f32[4]{0:T(128)} fusion(f32[4,64]{1,0:T(4,128)S(1)} %reshape.35, s32[]{:T(128)S(6)} %select_n.29), kind=kLoop, calls=%fused_computation.14 | loop fusion | bytes 36 | tf_op jit(solution)/shard_map/jit(dynamic_index_in_dim)/dynamic_slice | solution.py:290
  34.6 0.0 collective-permute-done
  34.6 0.0 copy-start
  34.7 0.0 copy-start.1
  34.7 0.0 copy-start.2
  34.7 0.0 copy-start.3
  34.7 0.2 fusion.query_ref
  34.9 7.4 %all-to-all-done = bf16[64,24,128]{2,1,0:T(8,128)(2,1)S(1)} async-done(((bf16[64,24,128]{2,1,0:T(8,128)(2,1)}), bf16[64,24,128]{2,1,0:T(8,128)(2,1)S(1)}, u32[]{:S(2)}, u32[]{:S(2)}) %all-to-all-start) | async-done | bytes 393248 | tf_op jit(solution)/shard_map/all_to_all | solution.py:257
  42.3 0.0 copy-done
  42.3 0.0 copy-done.1
  42.3 0.0 copy-done.2
  42.3 0.0 copy-done.3
  42.3 3.8 %filter.1 = bf16[640,128]{1,0:T(8,128)(2,1)S(1)} custom-call(bf16[1536,128]{1,0:T(8,128)(2,1)S(1)} %bitcast.13, f32[2,7,4]{2,1,0:T(8,128)} %copy.16.taps_ref, f32[4]{0:T(128)} %dynamic-slice_reduce_fusion.gain_ref, bf16[128,192]{1,0:T(8,128)(2,1)S(1)} %copy-done.2, bf16[64,384]{1,0:T(8,128)(2,1)S(1)} %copy-done.3, f32[2,64,256]{2,1,0:T(8,128)S(1)} %copy-done.1, ...), custom_call_target="tpu_custom_call" | custom-call | tf_op jit(solution)/shard_map/filter/pallas_call | solution.py:291
  46.1 20.3 %all_to_all.10 = bf16[64,5,2,128]{3,2,1,0:T(2,128)(2,1)S(1)} all-to-all(bf16[64,5,2,128]{3,2,1,0:T(2,128)(2,1)S(1)} %bitcast.14), channel_id=1, replica_groups={{272,336,400,464,16,80,144,208,280,344,408,472,24,88,152,216,288,352,41..., dimensions={0} | all-to-all | bytes 327680 | tf_op jit(solution)/shard_map/all_to_all | solution.py:257
  66.4 0.9 %finish.1 = bf16[256,256]{1,0:T(8,128)(2,1)} custom-call(bf16[640,128]{1,0:T(8,128)(2,1)S(1)} %bitcast.15, f32[256,256]{1,0:T(8,128)S(1)} %fusion.query_ref), custom_call_target="tpu_custom_call" | custom-call | tf_op jit(solution)/shard_map/finish/pallas_call | solution.py:303
  (3 shorter events, 0.0 us)
Async XLA Ops:
  8.1 21.3 %copy-start.4 = (bf16[256,256]{1,0:T(8,128)(2,1)S(1)}, bf16[256,256]{1,0:T(8,128)(2,1)}, u32[]{:S(2)}) copy-start(bf16[256,256]{1,0:T(8,128)(2,1)} %param.10) | copy-start | bytes 393220
  8.1 34.2 %all-to-all-start = ((bf16[64,24,128]{2,1,0:T(8,128)(2,1)}), bf16[64,24,128]{2,1,0:T(8,128)(2,1)S(1)}, u32[]{:S(2)}, u32[]{:S(2)}) async-start(bf16[64,24,128]{2,1,0:T(8,128)(2,1)} %bitcast.1), calls=%async_computation | async-start | bytes 786432 | tf_op jit(solution)/shard_map/all_to_all | solution.py:257
  29.4 5.2 %collective-permute-start = (bf16[6,256]{1,0:T(8,128)(2,1)S(1)}, bf16[6,256]{1,0:T(8,128)(2,1)S(1)}, u32[]{:S(2)}, u32[]{:S(2)}) collective-permute-start(bf16[6,256]{1,0:T(8,128)(2,1)S(1)} %slice.64), channel_id=1, source_target_pairs={{0,8},{8,16},{16,24},{24,32},{32,40},{40,48},{48,56},{56,64},{64,7... | collective-permute-start | bytes 9224 | tf_op jit(solution)/shard_map/ppermute | solution.py:270
  31.4 0.7 %slice-start = ((f32[3,7,256]{2,1,0:T(8,128)}), f32[2,7,256]{2,1,0:T(8,128)S(1)}, s32[]{:S(2)}) async-start(f32[3,7,256]{2,1,0:T(8,128)} %param.13), calls=%async_computation.2 | async-start | bytes 32768 | tf_op jit(solution)/shard_map/slice | solution.py:288
  32.1 0.7 %copy-start.5 = (f32[3,7,256]{2,1,0:T(8,128)S(1)}, f32[3,7,256]{2,1,0:T(8,128)}, u32[]{:S(2)}) copy-start(f32[3,7,256]{2,1,0:T(8,128)} %param.13) | copy-start | bytes 64516
  33.1 0.7 %copy-start.6 = (f32[256]{0:T(256)S(1)}, f32[256]{0:T(256)}, u32[]{:S(2)}) copy-start(f32[256]{0:T(256)} %param.15) | copy-start | bytes 3076
  34.6 7.7 %copy-start = (bf16[2,256,512]{2,1,0:T(8,128)(2,1)S(1)}, bf16[2,256,512]{2,1,0:T(8,128)(2,1)}, u32[]{:S(2)}) copy-start(bf16[2,256,512]{2,1,0:T(8,128)(2,1)} %constant.80.clone.inner_ref) | copy-start | bytes 1572868
  34.7 7.6 %copy-start.1 = (f32[2,64,256]{2,1,0:T(8,128)S(1)}, f32[2,64,256]{2,1,0:T(8,128)}, u32[]{:S(2)}) copy-start(f32[2,64,256]{2,1,0:T(8,128)} %constant.79.clone.twist_ref) | copy-start | bytes 393220
  34.7 7.6 %copy-start.2 = (bf16[128,192]{1,0:T(8,128)(2,1)S(1)}, bf16[128,192]{1,0:T(8,128)(2,1)}, u32[]{:S(2)}) copy-start(bf16[128,192]{1,0:T(8,128)(2,1)} %constant.77.clone.outer_ref) | copy-start | bytes 147460
  34.7 7.6 %copy-start.3 = (bf16[64,384]{1,0:T(8,128)(2,1)S(1)}, bf16[64,384]{1,0:T(8,128)(2,1)}, u32[]{:S(2)}) copy-start(bf16[64,384]{1,0:T(8,128)(2,1)} %constant.78.clone.back_ref) | copy-start | bytes 147460
